TPU v7x, 128 devices: a whole 4x4x4 slice. The times are simulated.
128 devices in a mesh: dp: 32 (over z, x, core), mp: 4 (over y).
Axes of the slice: x: 4, y: 4, z: 4, core: 2. Of those that a mesh axis runs over, the one named last changes fastest.
Arguments:
- hidden: bfloat16 [40960, 8192], P('dp', 'mp'), may hold values from -6 to 6
- rewards: float32 [256, 160], P('dp'), may hold values from -4 to 4
- lengths: int32 [256], P('dp'), may hold values from 1 to 160, as said below
- dest_shard: int32 [256], P('dp'), may hold values from 0 to 31, as said below
- source_owner: int32 [256], P('dp'), may hold values from 0 to 31, as said below
- pack_offset: int32 [256], P('dp'), may hold values from 0 to 639, as said below
- segment_ids: int32 [20480], P('dp'), may hold values from 0 to 7, as said below
- norm_gain: float32 [8192], replicated, may hold values from 0.5 to 1.5
- w_query: bfloat16 [8192, 4096], P(None, 'mp'), may hold values from -1 to 1
- w_key: bfloat16 [8192, 512], P(None, 'mp'), may hold values from -1 to 1
- w_value: bfloat16 [8192, 512], P(None, 'mp'), may hold values from -0.0625 to 0.0625
- value_head: float32 [8192], P('mp'), may hold values from -0.0625 to 0.0625
- folded_head: float32 [4096], P('mp'), may hold values from -0.09375 to 0.09375
Outputs:
- values: float32 [256, 160], P('dp')
- advantages: float32 [256, 160], P('dp')
Inputs may be any that keep to these rules, and one draw needn't show every extreme that they name: `lengths`: rows of a slot past its rollout's length are unused. Every critic shard holds a rollout of 160 rows. Some owner's 8 rollouts all have 160 rows. `dest_shard`: owner o packs its 8 rollouts on the shards o, o + 1, ..., o + 7, modulo the number of shards, one on each. `source_owner`: shard s packs one rollout from each of the owners s, s - 1, ..., s - 7, modulo the number of shards, in some order, agreeing with dest_shard. `pack_offset`: A shard's packed rollouts lie back to back in the order of their index, each with the length that lengths gives it, and fill all 640 rows. `segment_ids`: each packed row names the index of the packed rollout that holds it, as pack_offset and lengths lay them out.
All inputs are finite; a program needn't handle non-finite values.
Results may differ from a plain program's by a relative error of at most 0.007.
Values may be sent and summed in bfloat16 or wider, within the bound.
A program may use at most 192 MiB of HBM per device.

v0:
```python
import math

import jax
import jax.numpy as jnp
from jax import lax
from jax.sharding import PartitionSpec as P

HD = 128


EPSILON = 1e-05
DISCOUNT = 0.99
SMOOTHING = 0.95
ROPE_BASE = 500000.0


def passed_along(value, axis, by):
    length = lax.axis_size(axis)
    return lax.ppermute(value, axis, [(i, (i + by) % length) for i in range(length)])


def rotary(values_in, positions):
    half_width = values_in.shape[-1] // 2
    frequency = ROPE_BASE ** (-jnp.arange(half_width, dtype=jnp.float32) / half_width)
    angles = positions.astype(jnp.float32)[:, None] * frequency[None, :]
    cosine = jnp.cos(angles)[:, None, :]
    sine_part = jnp.sin(angles)[:, None, :]
    front_half = values_in[..., :half_width]
    back_half = values_in[..., half_width:]
    return jnp.concatenate(
        [front_half * cosine - back_half * sine_part, back_half * cosine + front_half * sine_part],
        axis=-1,
    )


def head_values(queries, keys_out, values_out, segments, positions, folded_head):
    row_count = queries.shape[0]
    kv_count = keys_out.shape[1] // HD
    group_size = queries.shape[1] // HD // kv_count
    query_rot = rotary(queries.reshape(row_count, kv_count * group_size, HD), positions).astype(
        jnp.bfloat16
    )
    query_rot = query_rot.reshape(row_count, kv_count, group_size, HD)
    key_rot = rotary(keys_out.reshape(row_count, kv_count, HD), positions).astype(jnp.bfloat16)
    value_rows = values_out.astype(jnp.bfloat16).reshape(row_count, kv_count, HD)
    scores = jnp.einsum(
        "qhgd,khd->hgqk", query_rot, key_rot, preferred_element_type=jnp.float32
    ) / math.sqrt(HD)
    allowed = (segments[:, None] == segments[None, :]) & (positions[:, None] >= positions[None, :])
    scores = jnp.where(allowed[None, None], scores, -1e30)
    row_max = jnp.max(scores, axis=-1, keepdims=True)
    exp_scores = jnp.where(allowed[None, None], jnp.exp(scores - row_max), 0.0)
    row_total = jnp.sum(exp_scores, axis=-1, keepdims=True)
    weights = (exp_scores / row_total).astype(jnp.bfloat16)
    attended = jnp.einsum("hgqk,khd->qhgd", weights, value_rows, preferred_element_type=jnp.float32)
    return jnp.sum(attended.reshape(row_count, -1) * folded_head[None, :], axis=1)


def local(
    hidden,
    rewards,
    lengths,
    dest_shard,
    source_owner,
    pack_offset,
    segment_ids,
    norm_gain,
    w_query,
    w_key,
    w_value,
    value_head,
    folded_head,
):
    shards = lax.axis_size("dp")
    shard_index = lax.axis_index("dp")
    rollouts = lengths.shape[0]
    slot_rows = rewards.shape[1]
    packed_rows = segment_ids.shape[0]
    part_width = hidden.shape[1]
    slot_lanes = jnp.arange(rollouts, dtype=jnp.int32)

    def slot_for(shift_by):
        target = (shard_index + shift_by) % shards
        return jnp.sum(jnp.where(dest_shard == target, slot_lanes, 0))

    def outgoing(shift_by, source):
        return lax.dynamic_slice_in_dim(source, slot_for(shift_by) * slot_rows, slot_rows, 0)

    source_step = (shard_index - source_owner) % shards
    lane_match = segment_ids[:, None] == slot_lanes[None, :]
    row_step = jnp.sum(jnp.where(lane_match, source_step[None, :], 0), axis=1)
    row_offset = jnp.sum(jnp.where(lane_match, pack_offset[None, :], 0), axis=1)
    positions = jnp.arange(packed_rows, dtype=jnp.int32) - row_offset
    pick_rows = row_step * slot_rows + positions
    full_rows = lax.all_gather(hidden, "mp", axis=1, tiled=True)
    received = [outgoing(0, full_rows)]
    for shift_by in range(1, rollouts):
        received.append(passed_along(outgoing(shift_by, full_rows), "dp", shift_by))
    packed = jnp.take(jnp.concatenate(received, axis=0), pick_rows, axis=0)
    packed_f = packed.astype(jnp.float32)
    row_scale = lax.rsqrt(jnp.mean(packed_f * packed_f, axis=1) + EPSILON)
    normed = (packed_f * row_scale[:, None] * norm_gain[None, :]).astype(jnp.bfloat16)
    queries = jnp.dot(normed, w_query, preferred_element_type=jnp.float32)
    keys_out = jnp.dot(normed, w_key, preferred_element_type=jnp.float32)
    values_out = jnp.dot(normed, w_value, preferred_element_type=jnp.float32)
    own_part = lax.dynamic_slice_in_dim(packed, lax.axis_index("mp") * part_width, part_width, 1)
    value_terms = head_values(queries, keys_out, values_out, segment_ids, positions, folded_head)
    value_terms = value_terms + jnp.sum(own_part.astype(jnp.float32) * value_head[None, :], axis=1)
    packed_values = lax.psum(value_terms, "mp")
    padded = jnp.concatenate([packed_values, jnp.zeros((slot_rows,), jnp.float32)])
    slot_values = jnp.zeros((rollouts, slot_rows), jnp.float32)
    for shift_by in range(rollouts):
        owner_now = (shard_index - shift_by) % shards
        j_index = jnp.sum(jnp.where(source_owner == owner_now, slot_lanes, 0))
        start_at = jnp.sum(jnp.where(slot_lanes == j_index, pack_offset, 0))
        arrived = lax.dynamic_slice_in_dim(padded, start_at, slot_rows, 0)
        if shift_by:
            arrived = passed_along(arrived, "dp", -shift_by)
        slot_values = jnp.where(
            (slot_lanes == slot_for(shift_by))[:, None], arrived[None, :], slot_values
        )
    step_ids = jnp.arange(slot_rows, dtype=jnp.int32)
    live_mask = step_ids[None, :] < lengths[:, None]
    values = jnp.where(live_mask, slot_values, 0.0)
    next_live = step_ids[None, :] + 1 < lengths[:, None]
    following = jnp.concatenate([values[:, 1:], jnp.zeros((rollouts, 1), jnp.float32)], axis=1)
    one_step = jnp.where(
        live_mask, rewards + DISCOUNT * jnp.where(next_live, following, 0.0) - values, 0.0
    )
    lag_matrix = (step_ids[:, None] - step_ids[None, :]).astype(jnp.float32)
    decay_table = jnp.where(
        lag_matrix >= 0, jnp.exp(lag_matrix * math.log(DISCOUNT * SMOOTHING)), 0.0
    )
    advantages = jnp.dot(one_step, decay_table, precision=lax.Precision.HIGHEST)
    return (values, advantages)


def solution(mesh):
    return jax.shard_map(
        local,
        mesh=mesh,
        in_specs=(
            P("dp", "mp"),
            P("dp", None),
            P("dp"),
            P("dp"),
            P("dp"),
            P("dp"),
            P("dp"),
            P(),
            P(None, "mp"),
            P(None, "mp"),
            P(None, "mp"),
            P("mp"),
            P("mp"),
        ),
        out_specs=(P("dp", None), P("dp", None)),
        check_vma=False,
    )
```

profile of v0, /device:TPU:1, one launch (start us, length us, event | category | flops | bytes accessed | tf_op | source)
XLA Modules:
  0.0 709.8 jit_solution(8402809665676939686)
XLA Ops:
  7.2 0.0 copy-start
  7.2 0.0 all-gather.2.cloned.1.call-start
  7.2 0.7 all-gather.2.cloned.1.call-update
  8.1 1.7 fusion.49
  15.0 187.3 %all-gather.2.cloned.1.call-done = bf16[1280,8192]{1,0:T(8,128)(2,1)} async-done(((bf16[1280,2048]{1,0:T(8,128)(2,1)}), bf16[1280,8192]{1,0:T(8,128)(2,1)}) %all-gather.2.cloned.1.call-update) | async-done | bytes 20971536 | tf_op jit(solution)/shard_map/all_gather | solution.py:95
  202.3 14.7 %constant_dynamic-slice_fusion = (bf16[160,8192]{1,0:T(8,128)(2,1)}, bf16[160,8192]{1,0:T(8,128)(2,1)}, bf16[160,8192]{1,0:T(8,128)(2,1)}, bf16[160,8192]{1,0:T(...) fusion(bf16[1280,8192]{1,0:T(8,128)(2,1)} %all-gather.2.cloned., ...), kind=kLoop, calls=%fused_computation.95 | loop fusion | bytes 41943072 | tf_op jit(solution)/shard_map/dynamic_slice | solution.py:87
  217.0 2.0 collective-permute-start
  219.0 5.7 fusion.58
  239.7 0.1 select_reduce_fusion.1
  239.8 0.7 iota_compare_fusion.10
  240.5 1.3 collective-permute-start.1
  241.7 0.7 iota_compare_fusion.3
  242.4 0.6 iota_compare_fusion.4
  243.0 0.7 iota_compare_fusion.5
  243.7 0.6 iota_compare_fusion.6
  244.4 0.7 iota_compare_fusion.7
  245.0 1.6 collective-permute-start.2
  246.6 0.4 compare_and_fusion
  247.0 1.2 multiply_cosine_fusion
  248.3 1.6 collective-permute-start.3
  249.9 3.0 collective-permute-start.4
  252.9 0.9 collective-permute-done
  253.8 2.5 collective-permute-start.5
  256.3 3.5 constant_dynamic-update-slice_fusion.6
  259.8 54.1 %collective-permute-done.1 = bf16[160,8192]{1,0:T(8,128)(2,1)S(1)} collective-permute-done((bf16[160,8192]{1,0:T(8,128)(2,1)}, bf16[160,8192]{1,0:T(8,128)(2,1)S(1)}, u32[]{:S(2)}, u32[]{:S(2)}) %collective-permute-start.1) | collective-permute-done | bytes 2621472 | tf_op jit(solution)/shard_map/ppermute | solution.py:19
  313.9 1.7 constant_dynamic-update-slice_fusion.5
  315.7 50.5 %collective-permute-done.2 = bf16[160,8192]{1,0:T(8,128)(2,1)S(1)} collective-permute-done((bf16[160,8192]{1,0:T(8,128)(2,1)}, bf16[160,8192]{1,0:T(8,128)(2,1)S(1)}, u32[]{:S(2)}, u32[]{:S(2)}) %collective-permute-start.2) | collective-permute-done | bytes 2621472 | tf_op jit(solution)/shard_map/ppermute | solution.py:19
  366.2 1.8 constant_dynamic-update-slice_fusion.4
  368.0 99.9 %collective-permute-done.3 = bf16[160,8192]{1,0:T(8,128)(2,1)S(1)} collective-permute-done((bf16[160,8192]{1,0:T(8,128)(2,1)}, bf16[160,8192]{1,0:T(8,128)(2,1)S(1)}, u32[]{:S(2)}, u32[]{:S(2)}) %collective-permute-start.3) | collective-permute-done | bytes 2621472 | tf_op jit(solution)/shard_map/ppermute | solution.py:19
  467.9 1.7 constant_dynamic-update-slice_fusion.3
  469.6 33.6 %collective-permute-done.4 = bf16[160,8192]{1,0:T(8,128)(2,1)S(1)} collective-permute-done((bf16[160,8192]{1,0:T(8,128)(2,1)}, bf16[160,8192]{1,0:T(8,128)(2,1)S(1)}, u32[]{:S(2)}, u32[]{:S(2)}) %collective-permute-start.4) | collective-permute-done | bytes 2621472 | tf_op jit(solution)/shard_map/ppermute | solution.py:19
  503.2 1.7 constant_dynamic-update-slice_fusion.2
  504.9 51.4 %collective-permute-done.5 = bf16[160,8192]{1,0:T(8,128)(2,1)S(1)} collective-permute-done((bf16[160,8192]{1,0:T(8,128)(2,1)}, bf16[160,8192]{1,0:T(8,128)(2,1)S(1)}, u32[]{:S(2)}, u32[]{:S(2)}) %collective-permute-start.5) | collective-permute-done | bytes 2621472 | tf_op jit(solution)/shard_map/ppermute | solution.py:19
  556.3 1.7 constant_dynamic-update-slice_fusion.1
  558.0 29.1 %collective-permute-done.6 = bf16[160,8192]{1,0:T(8,128)(2,1)S(1)} collective-permute-done((bf16[160,8192]{1,0:T(8,128)(2,1)}, bf16[160,8192]{1,0:T(8,128)(2,1)S(1)}, u32[]{:S(2)}, u32[]{:S(2)}) %collective-permute-start.6) | collective-permute-done | bytes 2621472 | tf_op jit(solution)/shard_map/ppermute | solution.py:19
  587.2 1.7 constant_dynamic-update-slice_fusion
  588.8 31.5 %gather_fusion = bf16[640,8192]{1,0:T(8,128)(2,1)} fusion(bf16[1280,8192]{1,0:T(8,128)(2,1)} %constant_dynamic-update-slice_fusion, s32[1024]{0:T(1024)S(1)} %pad_clamp_fusion), kind=kCustom, calls=%fused_computation | custom fusion | bytes 20974080 | tf_op jit(solution)/shard_map/jit(_take)/gather | solution.py:99
  620.3 7.7 %fusion = (f32[640]{0:T(1024)S(1)}, bf16[640,8192]{1,0:T(8,128)(2,1)S(1)}) fusion(bf16[640,8192]{1,0:T(8,128)(2,1)} %gather_fusion, pred[640]{0:T(1024)(128)(4,1)S(1)} %compare_and_fusion.1), kind=kLoop, calls=%fused_computation.3 | loop fusion | flops 20970880 | bytes 20974720 | tf_op jit(solution)/shard_map/reduce_sum | solution.py:101
  628.0 3.3 convolution_bitcast_fusion.1
  631.3 0.7 fusion.36
  632.0 14.4 %convolution_bitcast_fusion = f32[80,8,8,128]{3,1,2,0:T(8,128)S(1)} fusion(bf16[8192,1024]{1,0:T(8,128)(2,1)} %param.21, bf16[640,8192]{1,0:T(8,128)(2,1)S(1)} %get-tuple-element.29, f32[8192]{0:T(1024)S(1)} %copy-done.8, f32[640]{0:T(1024)S(1)} %add_rsqrt_fusion), kind=kOutput, calls=%fused_computation.20 | convolution fusion | flops 10758389760 | bytes 29919744 | tf_op jit(solution)/shard_map/dot_general | solution.py:103
  646.4 0.6 copy.35
  647.0 0.8 fusion.86
  647.9 1.0 subtract_convert_fusion
  648.9 6.4 fusion.3
  655.3 7.8 %fusion.4 = f32[8,640]{1,0:T(8,128)S(1)} fusion(f32[640,640,8]{1,0,2:T(8,128)} %get-tuple-element.58, f32[8,640]{1,0:T(8,128)S(1)} %get-tuple-element.57, pred[640,640]{0,1:T(8,128)(4,1)S(1)} %compare_and_fusion), kind=kLoop, calls=%fused_computation.11 | loop fusion | flops 16378880 | bytes 13557760 | tf_op jit(solution)/shard_map/reduce_sum | solution.py:53
  663.2 0.6 multiply_reduce_fusion
  663.8 0.0 copy-start.7
  663.8 0.0 copy-start.9
  663.8 14.8 %fusion.7 = f32[640]{0:T(1024)S(1)} fusion(f32[8,640]{1,0:T(8,128)S(1)} %fusion.4, f32[8,640]{1,0:T(8,128)S(1)} %get-tuple-element.57, f32[640,640,8]{1,0,2:T(8,128)} %get-tuple-element.58, pred[640,640]{0,1:T(8,128)(4,1)S(1)} %compare_and_fusion, f32[8,128]{1,0:T(8,128)S(1)} %bitcast.51, bf16[8192,128]{1,0:T(8,128)(2,1)} %param.23, ...), kind=kOutput, calls=%fused_computation.16 | convolution fusion | flops 2223062528 | bytes 26182656 | tf_op jit(solution)/shard_map/hgqk,khd->qhgd/dot_general | solution.py:55
  678.6 6.7 psum.7
  685.4 0.1 pad_dynamic-slice_fusion.7
  685.5 0.0 collective-permute-start.10
  685.5 0.1 collective-permute-start.11
  685.6 0.6 iota_compare_fusion.8
  686.2 9.0 %collective-permute-start.12 = (f32[160]{0:T(256)S(1)}, f32[160]{0:T(256)S(1)}, u32[]{:S(2)}, u32[]{:S(2)}) collective-permute-start(f32[160]{0:T(256)S(1)} %get-tuple-element.51), channel_id=1, source_target_pairs={{0,120},{4,124},{8,0},{12,4},{16,8},{20,12},{24,16},{28,20},{32,24... | collective-permute-start | bytes 1928 | tf_op jit(solution)/shard_map/ppermute | solution.py:19
  695.2 1.9 collective-permute-start.7
  697.2 0.6 collective-permute-start.9
  697.8 0.6 iota_compare_fusion.9
  698.4 2.4 collective-permute-done.8
  700.8 0.9 collective-permute-done.9
  701.7 0.1 select_select_fusion
  701.8 0.1 slice.26
  701.9 0.8 fusion.25
  (36 shorter events, 0.1 us)
Async XLA Ops:
  7.2 620.9 %copy-start = (bf16[8192,128]{1,0:T(8,128)(2,1)S(1)}, bf16[8192,128]{1,0:T(8,128)(2,1)}, u32[]{:S(2)}) copy-start(bf16[8192,128]{1,0:T(8,128)(2,1)} %param.22) | copy-start | bytes 6291460
  7.2 195.1 %all-gather.2.cloned.1.call-start = ((), (), s32[]{:S(2)}) async-start(), calls=%async_computation | async-start | bytes 26214400 | tf_op jit(solution)/shard_map/all_gather | solution.py:95
  14.9 204.1 %copy-start.6 = (s32[8]{0:T(128)S(1)}, s32[8]{0:T(128)}, u32[]{:S(2)}) copy-start(s32[8]{0:T(128)} %param.18) | copy-start | bytes 100
  15.0 224.7 %copy-start.3 = (s32[640]{0:T(1024)S(1)}, s32[640]{0:T(1024)}, u32[]{:S(2)}) copy-start(s32[640]{0:T(1024)} %param.19) | copy-start | bytes 7684
  217.0 36.8 %collective-permute-start = (bf16[160,8192]{1,0:T(8,128)(2,1)}, bf16[160,8192]{1,0:T(8,128)(2,1)}, u32[]{:S(2)}, u32[]{:S(2)}) collective-permute-start(bf16[160,8192]{1,0:T(8,128)(2,1)} %get-tuple-element.36), channel_id=1, source_target_pairs={{0,4},{4,8},{8,12},{12,16},{16,20},{20,24},{24,28},{28,32},{32,36}... | collective-permute-start | bytes 7864328 | tf_op jit(solution)/shard_map/ppermute | solution.py:19
  240.5 73.5 %collective-permute-start.1 = (bf16[160,8192]{1,0:T(8,128)(2,1)}, bf16[160,8192]{1,0:T(8,128)(2,1)S(1)}, u32[]{:S(2)}, u32[]{:S(2)}) collective-permute-start(bf16[160,8192]{1,0:T(8,128)(2,1)} %get-tuple-element.35), channel_id=1, source_target_pairs={{0,8},{4,12},{8,16},{12,20},{16,24},{20,28},{24,32},{28,36},{32,40... | collective-permute-start | bytes 7864328 | tf_op jit(solution)/shard_map/ppermute | solution.py:19
  245.0 121.1 %collective-permute-start.2 = (bf16[160,8192]{1,0:T(8,128)(2,1)}, bf16[160,8192]{1,0:T(8,128)(2,1)S(1)}, u32[]{:S(2)}, u32[]{:S(2)}) collective-permute-start(bf16[160,8192]{1,0:T(8,128)(2,1)} %get-tuple-element.34), channel_id=1, source_target_pairs={{0,12},{4,16},{8,20},{12,24},{16,28},{20,32},{24,36},{28,40},{32,4... | collective-permute-start | bytes 7864328 | tf_op jit(solution)/shard_map/ppermute | solution.py:19
  248.3 219.6 %collective-permute-start.3 = (bf16[160,8192]{1,0:T(8,128)(2,1)}, bf16[160,8192]{1,0:T(8,128)(2,1)S(1)}, u32[]{:S(2)}, u32[]{:S(2)}) collective-permute-start(bf16[160,8192]{1,0:T(8,128)(2,1)} %get-tuple-element.33), channel_id=1, source_target_pairs={{0,16},{4,20},{8,24},{12,28},{16,32},{20,36},{24,40},{28,44},{32,4... | collective-permute-start | bytes 7864328 | tf_op jit(solution)/shard_map/ppermute | solution.py:19
  249.9 253.3 %collective-permute-start.4 = (bf16[160,8192]{1,0:T(8,128)(2,1)}, bf16[160,8192]{1,0:T(8,128)(2,1)S(1)}, u32[]{:S(2)}, u32[]{:S(2)}) collective-permute-start(bf16[160,8192]{1,0:T(8,128)(2,1)} %get-tuple-element.32), channel_id=1, source_target_pairs={{0,20},{4,24},{8,28},{12,32},{16,36},{20,40},{24,44},{28,48},{32,5... | collective-permute-start | bytes 7864328 | tf_op jit(solution)/shard_map/ppermute | solution.py:19
  253.8 302.5 %collective-permute-start.5 = (bf16[160,8192]{1,0:T(8,128)(2,1)}, bf16[160,8192]{1,0:T(8,128)(2,1)S(1)}, u32[]{:S(2)}, u32[]{:S(2)}) collective-permute-start(bf16[160,8192]{1,0:T(8,128)(2,1)} %get-tuple-element.31), channel_id=1, source_target_pairs={{0,24},{4,28},{8,32},{12,36},{16,40},{20,44},{24,48},{28,52},{32,5... | collective-permute-start | bytes 7864328 | tf_op jit(solution)/shard_map/ppermute | solution.py:19
  313.9 273.2 %collective-permute-start.6 = (bf16[160,8192]{1,0:T(8,128)(2,1)}, bf16[160,8192]{1,0:T(8,128)(2,1)S(1)}, u32[]{:S(2)}, u32[]{:S(2)}) collective-permute-start(bf16[160,8192]{1,0:T(8,128)(2,1)} %get-tuple-element.30), channel_id=1, source_target_pairs={{0,28},{4,32},{8,36},{12,40},{16,44},{20,48},{24,52},{28,56},{32,6... | collective-permute-start | bytes 7864328 | tf_op jit(solution)/shard_map/ppermute | solution.py:19
  620.3 7.7 %copy-start.8 = (f32[8192]{0:T(1024)S(1)}, f32[8192]{0:T(1024)}, u32[]{:S(2)}) copy-start(f32[8192]{0:T(1024)} %param.20) | copy-start | bytes 98308
  628.0 35.1 %copy-start.2 = (bf16[640,8192]{1,0:T(8,128)(2,1)}, bf16[640,8192]{1,0:T(8,128)(2,1)S(1)}, u32[]{:S(2)}) copy-start(bf16[640,8192]{1,0:T(8,128)(2,1)S(1)} %get-tuple-element.29) | copy-start | bytes 31457284
  655.3 7.9 %copy-start.5 = (f32[2048]{0:T(1024)S(1)}, f32[2048]{0:T(1024)}, u32[]{:S(2)}) copy-start(f32[2048]{0:T(1024)} %param.24) | copy-start | bytes 24580
  655.3 8.5 %copy-start.10 = (f32[1024]{0:T(1024)S(1)}, f32[1024]{0:T(1024)}, u32[]{:S(2)}) copy-start(f32[1024]{0:T(1024)} %param.25) | copy-start | bytes 12292
  663.8 37.9 %copy-start.7 = (s32[8]{0:T(128)S(1)}, s32[8]{0:T(128)}, u32[]{:S(2)}) copy-start(s32[8]{0:T(128)} %param.15) | copy-start | bytes 100
  663.8 38.1 %copy-start.9 = (f32[8,160]{1,0:T(8,128)S(1)}, f32[8,160]{1,0:T(8,128)}, u32[]{:S(2)}) copy-start(f32[8,160]{1,0:T(8,128)} %param.14) | copy-start | bytes 15364
  663.8 38.9 %copy-start.1 = (bf16[8192,128]{1,0:T(8,128)(2,1)S(1)}, bf16[8192,128]{1,0:T(8,128)(2,1)}, u32[]{:S(2)}) copy-start(bf16[8192,128]{1,0:T(8,128)(2,1)} %param.22) | copy-start | bytes 6291460
  685.5 11.7 %collective-permute-start.10 = (f32[160]{0:T(256)S(1)}, f32[160]{0:T(256)S(1)}, u32[]{:S(2)}, u32[]{:S(2)}) collective-permute-start(f32[160]{0:T(256)S(1)} %get-tuple-element.49), channel_id=1, source_target_pairs={{0,112},{4,116},{8,120},{12,124},{16,0},{20,4},{24,8},{28,12},{32,... | collective-permute-start | bytes 1928 | tf_op jit(solution)/shard_map/ppermute | solution.py:19
  685.5 11.7 %collective-permute-start.11 = (f32[160]{0:T(256)S(1)}, f32[160]{0:T(256)S(1)}, u32[]{:S(2)}, u32[]{:S(2)}) collective-permute-start(f32[160]{0:T(256)S(1)} %get-tuple-element.50), channel_id=1, source_target_pairs={{0,116},{4,120},{8,124},{12,0},{16,4},{20,8},{24,12},{28,16},{32,2... | collective-permute-start | bytes 1928 | tf_op jit(solution)/shard_map/ppermute | solution.py:19
  686.2 12.1 %collective-permute-start.12 = (f32[160]{0:T(256)S(1)}, f32[160]{0:T(256)S(1)}, u32[]{:S(2)}, u32[]{:S(2)}) collective-permute-start(f32[160]{0:T(256)S(1)} %get-tuple-element.51), channel_id=1, source_target_pairs={{0,120},{4,124},{8,0},{12,4},{16,8},{20,12},{24,16},{28,20},{32,24... | collective-permute-start | bytes 1928 | tf_op jit(solution)/shard_map/ppermute | solution.py:19
  695.2 3.1 collective-permute-start.13
  695.2 3.1 collective-permute-start.7
  697.2 3.6 collective-permute-start.8
  697.2 4.5 collective-permute-start.9
  701.8 0.9 copy-start.4
Sparse Core Ops, SparseCore 0:
  9.7 192.5 all-gather.1
where the time goes:
time: 718 us; the launch traced here: 710 us
  waiting for transfers between devices  511 us (71%)
  local copies, waits for them, and re-layouts  61.7 us (9%)
  matrix products  39.7 us (6%)
  between operations  34.9 us (5%)
  other arithmetic  32.1 us (4%)
  starting transfers between devices  23.6 us (3%)
    ppermute x14, waiting for transfers between devices, passed_along(): lax.ppermute(value, axis, [(i, (i + by) % length) for i in range(length)])  323 us
    all_gather x1, waiting for transfers between devices, local(): full_rows = lax.all_gather(hidden, 'mp', axis=1, tiled=True)  187 us
    gather x1, local copies, waits for them, and re-layouts, local(): packed = jnp.take(jnp.concatenate(received, axis=0), pick_rows, axis=0)  31.5 us
    ppermute x14, starting transfers between devices, passed_along(): lax.ppermute(value, axis, [(i, (i + by) % length) for i in range(length)])  23.6 us
    dot_general x1, matrix products, head_values(): jnp.einsum('hgqk,khd->qhgd', weights, value_rows, preferred_element_type=...  14.8 us
    dynamic_slice x1, local copies, waits for them, and re-layouts, outgoing(): lax.dynamic_slice_in_dim(source, slot_for(shift_by) * slot_rows, slot_row...  14.7 us
    dot_general x1, matrix products, local(): queries = jnp.dot(normed, w_query, preferred_element_type=jnp.float32)  14.4 us
  transfers between devices with their start and end apart: 15, of which 10 were waited for; matrix products, arithmetic and copies ran while one was open for 4% of the time, Pallas kernels for 0%

commit v1 on v0

--- a/solution.py
+++ b/solution.py
@@ -76,7 +76,6 @@
     rollouts = lengths.shape[0]
     slot_rows = rewards.shape[1]
     packed_rows = segment_ids.shape[0]
-    part_width = hidden.shape[1]
     slot_lanes = jnp.arange(rollouts, dtype=jnp.int32)
 
     def slot_for(shift_by):
@@ -92,18 +91,17 @@
     row_offset = jnp.sum(jnp.where(lane_match, pack_offset[None, :], 0), axis=1)
     positions = jnp.arange(packed_rows, dtype=jnp.int32) - row_offset
     pick_rows = row_step * slot_rows + positions
-    full_rows = lax.all_gather(hidden, "mp", axis=1, tiled=True)
-    received = [outgoing(0, full_rows)]
+    received = [outgoing(0, hidden)]
     for shift_by in range(1, rollouts):
-        received.append(passed_along(outgoing(shift_by, full_rows), "dp", shift_by))
-    packed = jnp.take(jnp.concatenate(received, axis=0), pick_rows, axis=0)
+        received.append(passed_along(outgoing(shift_by, hidden), "dp", shift_by))
+    own_part = jnp.take(jnp.concatenate(received, axis=0), pick_rows, axis=0)
+    packed = lax.all_gather(own_part, "mp", axis=1, tiled=True)
     packed_f = packed.astype(jnp.float32)
     row_scale = lax.rsqrt(jnp.mean(packed_f * packed_f, axis=1) + EPSILON)
     normed = (packed_f * row_scale[:, None] * norm_gain[None, :]).astype(jnp.bfloat16)
     queries = jnp.dot(normed, w_query, preferred_element_type=jnp.float32)
     keys_out = jnp.dot(normed, w_key, preferred_element_type=jnp.float32)
     values_out = jnp.dot(normed, w_value, preferred_element_type=jnp.float32)
-    own_part = lax.dynamic_slice_in_dim(packed, lax.axis_index("mp") * part_width, part_width, 1)
     value_terms = head_values(queries, keys_out, values_out, segment_ids, positions, folded_head)
     value_terms = value_terms + jnp.sum(own_part.astype(jnp.float32) * value_head[None, :], axis=1)
     packed_values = lax.psum(value_terms, "mp")

time: 718 us -> 325 us (0.45); the launches traced: 710 us -> 324 us
  waiting for transfers between devices: 511 us -> 149 us
  local copies, waits for them, and re-layouts: 61.7 us -> 22.7 us
  other arithmetic: 32.1 us -> 42 us
    ppermute x14, waiting for transfers between devices: 323 us -> 79.7 us  [passed_along(): lax.ppermute(value, axis, [(i, (i + by) % length) for i in range(length)])]
    all_gather x1, waiting for transfers between devices: 187 us -> 69.3 us  [local(): packed = lax.all_gather(own_part, 'mp', axis=1, tiled=True)]
    gather x1, local copies, waits for them, and re-layouts: 31.5 us -> 10.1 us  [local(): own_part = jnp.take(jnp.concatenate(received, axis=0), pick_rows, axis=0)]
    dynamic_slice x1, local copies, waits for them, and re-layouts: 14.7 us -> 3.8 us  [outgoing(): lax.dynamic_slice_in_dim(source, slot_for(shift_by) * slot_rows, slot_row...]
  transfers between devices with their start and end apart: 15 -> 15, of which waited for: 10 -> 9; matrix products, arithmetic and copies ran while one was open for 4% -> 7% of each run, Pallas kernels for 0% -> 0%
where the time goes in v1:
time: 325 us; the launch traced here: 324 us
  waiting for transfers between devices  149 us (46%)
  other arithmetic  42 us (13%)
  matrix products  41.8 us (13%)
  between operations  34.6 us (11%)
  starting transfers between devices  27 us (8%)
  local copies, waits for them, and re-layouts  22.7 us (7%)
  blocking collectives  7.21 us (2%)
    ppermute x14, waiting for transfers between devices, passed_along(): lax.ppermute(value, axis, [(i, (i + by) % length) for i in range(length)])  79.7 us
    all_gather x1, waiting for transfers between devices, local(): packed = lax.all_gather(own_part, 'mp', axis=1, tiled=True)  69.3 us
    ppermute x14, starting transfers between devices, passed_along(): lax.ppermute(value, axis, [(i, (i + by) % length) for i in range(length)])  27 us
    dot_general x1, matrix products, head_values(): jnp.einsum('hgqk,khd->qhgd', weights, value_rows, preferred_element_type=...  14.9 us
    dot_general x1, matrix products, local(): queries = jnp.dot(normed, w_query, preferred_element_type=jnp.float32)  14.8 us
    gather x1, local copies, waits for them, and re-layouts, local(): own_part = jnp.take(jnp.concatenate(received, axis=0), pick_rows, axis=0)  10.1 us
    eq x8, other arithmetic, local(): slot_lanes == slot_for(shift_by)  8.29 us
    reduce_sum x1, other arithmetic, head_values(): row_total = jnp.sum(exp_scores, axis=-1, keepdims=True)  7.83 us
  transfers between devices with their start and end apart: 15, of which 9 were waited for; matrix products, arithmetic and copies ran while one was open for 7% of the time, Pallas kernels for 0%

profile of v1, /device:TPU:1, one launch (start us, length us, event | category | flops | bytes accessed | tf_op | source)
XLA Modules:
  0.0 324.4 jit_solution(14331908132062440243)
XLA Ops:
  7.2 0.0 all-gather.2.cloned.1.call-start
  7.4 1.9 fusion.49
  14.4 3.8 %constant_dynamic-slice_fusion = (bf16[160,2048]{1,0:T(8,128)(2,1)S(1)}, bf16[160,2048]{1,0:T(8,128)(2,1)S(1)}, bf16[160,2048]{1,0:T(8,128)(2,1)S(1)}, bf16[160,...) fusion(bf16[1280,2048]{1,0:T(8,128)(2,1)} %param.13, ...), kind=kLoop, calls=%fused_computation.98 | loop fusion | bytes 10485792 | tf_op jit(solution)/shard_map/dynamic_slice | solution.py:86
  18.2 2.6 collective-permute-start
  20.8 1.2 collective-permute-start.1
  22.0 1.5 collective-permute-start.2
  23.5 1.9 collective-permute-start.3
  25.4 3.4 %collective-permute-start.4 = (bf16[160,2048]{1,0:T(8,128)(2,1)S(1)}, bf16[160,2048]{1,0:T(8,128)(2,1)S(1)}, u32[]{:S(2)}, u32[]{:S(2)}) collective-permute-start(bf16[160,2048]{1,0:T(8,128)(2,1)S(1)} %get-tuple-element.33), channel_id=1, source_target_pairs={{0,20},{4,24},{8,28},{12,32},{16,36},{20,40},{24,44},{28,48},{32,5... | collective-permute-start | bytes 1966088 | tf_op jit(solution)/shard_map/ppermute | solution.py:19
  28.8 0.1 select_reduce_fusion.1
  28.9 5.8 %collective-permute-done = bf16[160,2048]{1,0:T(8,128)(2,1)S(1)} collective-permute-done((bf16[160,2048]{1,0:T(8,128)(2,1)S(1)}, bf16[160,2048]{1,0:T(8,128)(2,1)S(1)}, u32[]{:S(2)}, u32[]{:S(2)}) %collective-permute-start) | collective-permute-done | bytes 655392 | tf_op jit(solution)/shard_map/ppermute | solution.py:19
  34.8 2.8 collective-permute-start.5
  37.6 0.9 constant_dynamic-update-slice_fusion.6
  38.5 14.7 %collective-permute-done.1 = bf16[160,2048]{1,0:T(8,128)(2,1)S(1)} collective-permute-done((bf16[160,2048]{1,0:T(8,128)(2,1)S(1)}, bf16[160,2048]{1,0:T(8,128)(2,1)S(1)}, u32[]{:S(2)}, u32[]{:S(2)}) %collective-permute-start.1) | collective-permute-done | bytes 655392 | tf_op jit(solution)/shard_map/ppermute | solution.py:19
  53.1 0.9 constant_dynamic-update-slice_fusion.5
  54.1 8.8 %collective-permute-done.2 = bf16[160,2048]{1,0:T(8,128)(2,1)S(1)} collective-permute-done((bf16[160,2048]{1,0:T(8,128)(2,1)S(1)}, bf16[160,2048]{1,0:T(8,128)(2,1)S(1)}, u32[]{:S(2)}, u32[]{:S(2)}) %collective-permute-start.2) | collective-permute-done | bytes 655392 | tf_op jit(solution)/shard_map/ppermute | solution.py:19
  62.8 0.9 constant_dynamic-update-slice_fusion.4
  63.8 35.7 %collective-permute-done.3 = bf16[160,2048]{1,0:T(8,128)(2,1)S(1)} collective-permute-done((bf16[160,2048]{1,0:T(8,128)(2,1)S(1)}, bf16[160,2048]{1,0:T(8,128)(2,1)S(1)}, u32[]{:S(2)}, u32[]{:S(2)}) %collective-permute-start.3) | collective-permute-done | bytes 655392 | tf_op jit(solution)/shard_map/ppermute | solution.py:19
  99.4 0.9 constant_dynamic-update-slice_fusion.3
  100.3 0.0 collective-permute-done.4
  100.4 0.9 constant_dynamic-update-slice_fusion.2
  101.3 7.6 %collective-permute-done.5 = bf16[160,2048]{1,0:T(8,128)(2,1)S(1)} collective-permute-done((bf16[160,2048]{1,0:T(8,128)(2,1)S(1)}, bf16[160,2048]{1,0:T(8,128)(2,1)S(1)}, u32[]{:S(2)}, u32[]{:S(2)}) %collective-permute-start.5) | collective-permute-done | bytes 655392 | tf_op jit(solution)/shard_map/ppermute | solution.py:19
  108.9 0.9 constant_dynamic-update-slice_fusion.1
  109.8 5.4 %collective-permute-done.6 = bf16[160,2048]{1,0:T(8,128)(2,1)S(1)} collective-permute-done((bf16[160,2048]{1,0:T(8,128)(2,1)S(1)}, bf16[160,2048]{1,0:T(8,128)(2,1)S(1)}, u32[]{:S(2)}, u32[]{:S(2)}) %collective-permute-start.6) | collective-permute-done | bytes 655392 | tf_op jit(solution)/shard_map/ppermute | solution.py:19
  115.1 0.9 constant_dynamic-update-slice_fusion
  116.0 10.1 %gather_fusion = bf16[640,2048]{1,0:T(8,128)(2,1)} fusion(bf16[1280,2048]{1,0:T(8,128)(2,1)} %constant_dynamic-update-slice_fusion, s32[1024]{0:T(1024)S(1)} %pad_clamp_fusion), kind=kCustom, calls=%fused_computation | custom fusion | bytes 5245440 | tf_op jit(solution)/shard_map/jit(_take)/gather | solution.py:97
  126.1 4.1 %multiply_reduce_fusion = (f32[640]{0:T(1024)S(1)}, bf16[640,2048]{1,0:T(8,128)(2,1)}) fusion(f32[2048]{0:T(1024)S(1)} %copy-done.6, bf16[640,2048]{1,0:T(8,128)(2,1)} %gather_fusion, pred[640]{0:T(1024)(128)(4,1)S(1)} %compare_and_fusion.1), kind=kLoop, calls=%fused_computation.13 | loop fusion | flops 5242240 | bytes 5254272 | tf_op jit(solution)/shard_map/reduce_sum | solution.py:106
  130.2 5.9 %fusion.58 = (s32[]{:T(128)}, s32[]{:T(128)}, s32[]{:T(128)}, s32[]{:T(128)}, s32[]{:T(128)}, /*index=5*/s32[]{:T(128)}, s32[]{:T(128)}, s32[]{:T(128)}) fusion(s32[8]{0:T(128)S(1)} %copy-done.7, s32[]{:T(128)} %get-tuple-element.67, s32[]{:T(128)} %get-tuple-element.66, s32[]{:T(128)} %get-tuple-element.65, s32[]{:T(128)} %get-tuple-element.64, ...), kind=kLoop, calls=%fused_computation.140 | loop fusion | flops 184 | bytes 96 | tf_op jit(solution)/shard_map/reduce_sum | solution.py:113
  151.1 1.3 iota_compare_fusion.3
  152.4 1.2 iota_compare_fusion.4
  153.6 1.1 iota_compare_fusion.5
  154.7 1.2 iota_compare_fusion.6
  155.9 1.2 iota_compare_fusion.7
  157.0 1.2 iota_compare_fusion.8
  158.2 0.6 iota_add_fusion
  158.8 1.1 compare_and_fusion
  159.9 2.0 multiply_cosine_fusion
  161.9 69.3 %all-gather.2.cloned.1.call-done = bf16[640,8192]{1,0:T(8,128)(2,1)} async-done(((bf16[640,2048]{1,0:T(8,128)(2,1)}), bf16[640,8192]{1,0:T(8,128)(2,1)}) %all-gather.2.cloned.1.call-update) | async-done | bytes 10485776 | tf_op jit(solution)/shard_map/all_gather | solution.py:98
  231.2 6.2 %fusion = f32[640]{0:T(1024)S(1)} fusion(bf16[640,8192]{1,0:T(8,128)(2,1)} %all-gather.2.cloned.1.call-done), kind=kLoop, calls=%fused_computation.3 | loop fusion | flops 15728000 | bytes 10488320 | tf_op jit(solution)/shard_map/reduce_sum | solution.py:100
  237.5 0.7 copy-done.2
  238.2 14.8 %convolution_bitcast_fusion = f32[80,8,8,128]{3,1,2,0:T(8,128)S(1)} fusion(bf16[8192,1024]{1,0:T(8,128)(2,1)} %param.21, bf16[640,8192]{1,0:T(8,128)(2,1)S(1)} %copy-done.2, f32[8192]{0:T(1024)} %param.20, f32[640]{0:T(1024)S(1)} %add_rsqrt_fusion), kind=kOutput, calls=%fused_computation.19 | convolution fusion | flops 10758389760 | bytes 29919744 | tf_op jit(solution)/shard_map/dot_general | solution.py:102
  253.0 0.6 copy.35
  253.6 0.8 fusion.86
  254.5 4.9 %convolution_bitcast_fusion.1 = f32[640,1,128]{0,2,1:T(8,128)} fusion(bf16[8192,128]{1,0:T(8,128)(2,1)S(1)} %copy-done, bf16[640,8192]{1,0:T(8,128)(2,1)S(1)} %copy-done.2, f32[8192]{0:T(1024)} %param.20, f32[640]{0:T(1024)S(1)} %add_rsqrt_fusion), kind=kOutput, calls=%fused_computation.25 | convolution fusion | flops 1363148800 | bytes 12945920 | tf_op jit(solution)/shard_map/dot_general | solution.py:103
  259.3 1.7 fusion.36
  261.1 2.1 subtract_convert_fusion
  263.2 6.4 %fusion.3 = (f32[8,640]{1,0:T(8,128)S(1)}, f32[640,640,8]{1,0,2:T(8,128)}) fusion(pred[640,640]{0,1:T(8,128)(4,1)S(1)} %copy-done.3, bf16[640,8,64]{2,0,1:T(8,128)(2,1)S(1)} %get-tuple-element.31, bf16[640,8,64]{2,0,1:T(8,128)(2,1)S(1)} %get-tuple-element.30, bf16[640,64]{0,1:T(8,128)(2,1)S(1)} %get-tuple-element.43, bf16[640,64]{0,1:T(8,128)(2,1)S(1)} %get-tuple-element.42), kind=kOutput, calls=%fused_computation.9 | convolution fusion | flops 851635200 | bytes 15011840 | tf_op jit(solution)/shard_map/qhgd,khd->hgqk/dot_general | solution.py:46
  269.6 7.8 %fusion.4 = f32[8,640]{1,0:T(8,128)S(1)} fusion(f32[640,640,8]{1,0,2:T(8,128)} %get-tuple-element.58, f32[8,640]{1,0:T(8,128)S(1)} %get-tuple-element.57, pred[640,640]{0,1:T(8,128)(4,1)S(1)} %copy-done.3), kind=kLoop, calls=%fused_computation.10 | loop fusion | flops 16378880 | bytes 13557760 | tf_op jit(solution)/shard_map/reduce_sum | solution.py:53
  277.5 14.9 %fusion.7 = f32[640]{0:T(1024)S(1)} fusion(f32[8,640]{1,0:T(8,128)S(1)} %fusion.4, f32[8,640]{1,0:T(8,128)S(1)} %get-tuple-element.57, f32[640,640,8]{1,0,2:T(8,128)} %get-tuple-element.58, pred[640,640]{0,1:T(8,128)(4,1)S(1)} %copy-done.3, f32[8,128]{1,0:T(8,128)S(1)} %bitcast.51, bf16[8192,128]{1,0:T(8,128)(2,1)} %param.23, ...), kind=kOutput, calls=%fused_computation.15 | convolution fusion | flops 2223062528 | bytes 26182656 | tf_op jit(solution)/shard_map/hgqk,khd->qhgd/dot_general | solution.py:55
  292.4 7.2 %psum.7 = f32[640]{0:T(1024)S(1)} all-reduce(f32[640]{0:T(1024)S(1)} %add.252), channel_id=1, replica_groups=mesh['dp'=32,'mp'=4] {'mp'}, use_global_device_ids=true, to_apply=%region_15.16 | all-reduce | flops 640 | bytes 5120 | tf_op jit(solution)/shard_map/psum | solution.py:107
  299.7 0.1 pad_dynamic-slice_fusion.7
  299.8 3.0 collective-permute-start.13
  302.7 5.0 %collective-permute-start.12 = (f32[160]{0:T(256)S(1)}, f32[160]{0:T(256)S(1)}, u32[]{:S(2)}, u32[]{:S(2)}) collective-permute-start(f32[160]{0:T(256)S(1)} %get-tuple-element.51), channel_id=1, source_target_pairs={{0,120},{4,124},{8,0},{12,4},{16,8},{20,12},{24,16},{28,20},{32,24... | collective-permute-start | bytes 1928 | tf_op jit(solution)/shard_map/ppermute | solution.py:19
  307.7 0.6 iota_compare_fusion.9
  308.3 0.9 collective-permute-start.11
  309.2 0.3 collective-permute-start.10
  309.5 3.1 collective-permute-start.9
  312.6 0.5 collective-permute-start.8
  313.1 0.8 collective-permute-start.7
  313.9 0.6 iota_compare_fusion.10
  314.6 1.7 collective-permute-done.8
  316.3 0.1 collective-permute-done.7
  316.5 0.1 select_select_fusion
  316.6 0.1 slice.26
  316.7 0.8 fusion.25
  (54 shorter events, 0.2 us)
Async XLA Ops:
  7.2 247.3 %copy-start = (bf16[8192,128]{1,0:T(8,128)(2,1)S(1)}, bf16[8192,128]{1,0:T(8,128)(2,1)}, u32[]{:S(2)}) copy-start(bf16[8192,128]{1,0:T(8,128)(2,1)} %param.22) | copy-start | bytes 6291460
  7.2 224.0 %all-gather.2.cloned.1.call-start = ((), (), s32[]{:S(2)}) async-start(), calls=%async_computation | async-start | bytes 13107200 | tf_op jit(solution)/shard_map/all_gather | solution.py:98
  14.4 14.4 %copy-start.4 = (s32[640]{0:T(1024)S(1)}, s32[640]{0:T(1024)}, u32[]{:S(2)}) copy-start(s32[640]{0:T(1024)} %param.19) | copy-start | bytes 7684
  14.4 14.4 %copy-start.7 = (s32[8]{0:T(128)S(1)}, s32[8]{0:T(128)}, u32[]{:S(2)}) copy-start(s32[8]{0:T(128)} %param.18) | copy-start | bytes 100
  18.2 16.6 %collective-permute-start = (bf16[160,2048]{1,0:T(8,128)(2,1)S(1)}, bf16[160,2048]{1,0:T(8,128)(2,1)S(1)}, u32[]{:S(2)}, u32[]{:S(2)}) collective-permute-start(bf16[160,2048]{1,0:T(8,128)(2,1)S(1)} %get-tuple-element.37), channel_id=1, source_target_pairs={{0,4},{4,8},{8,12},{12,16},{16,20},{20,24},{24,28},{28,32},{32,36}... | collective-permute-start | bytes 1966088 | tf_op jit(solution)/shard_map/ppermute | solution.py:19
  20.8 32.4 %collective-permute-start.1 = (bf16[160,2048]{1,0:T(8,128)(2,1)S(1)}, bf16[160,2048]{1,0:T(8,128)(2,1)S(1)}, u32[]{:S(2)}, u32[]{:S(2)}) collective-permute-start(bf16[160,2048]{1,0:T(8,128)(2,1)S(1)} %get-tuple-element.36), channel_id=1, source_target_pairs={{0,8},{4,12},{8,16},{12,20},{16,24},{20,28},{24,32},{28,36},{32,40... | collective-permute-start | bytes 1966088 | tf_op jit(solution)/shard_map/ppermute | solution.py:19
  22.0 40.8 %collective-permute-start.2 = (bf16[160,2048]{1,0:T(8,128)(2,1)S(1)}, bf16[160,2048]{1,0:T(8,128)(2,1)S(1)}, u32[]{:S(2)}, u32[]{:S(2)}) collective-permute-start(bf16[160,2048]{1,0:T(8,128)(2,1)S(1)} %get-tuple-element.35), channel_id=1, source_target_pairs={{0,12},{4,16},{8,20},{12,24},{16,28},{20,32},{24,36},{28,40},{32,4... | collective-permute-start | bytes 1966088 | tf_op jit(solution)/shard_map/ppermute | solution.py:19
  23.5 75.9 %collective-permute-start.3 = (bf16[160,2048]{1,0:T(8,128)(2,1)S(1)}, bf16[160,2048]{1,0:T(8,128)(2,1)S(1)}, u32[]{:S(2)}, u32[]{:S(2)}) collective-permute-start(bf16[160,2048]{1,0:T(8,128)(2,1)S(1)} %get-tuple-element.34), channel_id=1, source_target_pairs={{0,16},{4,20},{8,24},{12,28},{16,32},{20,36},{24,40},{28,44},{32,4... | collective-permute-start | bytes 1966088 | tf_op jit(solution)/shard_map/ppermute | solution.py:19
  25.4 75.0 %collective-permute-start.4 = (bf16[160,2048]{1,0:T(8,128)(2,1)S(1)}, bf16[160,2048]{1,0:T(8,128)(2,1)S(1)}, u32[]{:S(2)}, u32[]{:S(2)}) collective-permute-start(bf16[160,2048]{1,0:T(8,128)(2,1)S(1)} %get-tuple-element.33), channel_id=1, source_target_pairs={{0,20},{4,24},{8,28},{12,32},{16,36},{20,40},{24,44},{28,48},{32,5... | collective-permute-start | bytes 1966088 | tf_op jit(solution)/shard_map/ppermute | solution.py:19
  34.8 74.1 %collective-permute-start.5 = (bf16[160,2048]{1,0:T(8,128)(2,1)S(1)}, bf16[160,2048]{1,0:T(8,128)(2,1)S(1)}, u32[]{:S(2)}, u32[]{:S(2)}) collective-permute-start(bf16[160,2048]{1,0:T(8,128)(2,1)S(1)} %get-tuple-element.39), channel_id=1, source_target_pairs={{0,24},{4,28},{8,32},{12,36},{16,40},{20,44},{24,48},{28,52},{32,5... | collective-permute-start | bytes 1966088 | tf_op jit(solution)/shard_map/ppermute | solution.py:19
  53.1 62.0 %collective-permute-start.6 = (bf16[160,2048]{1,0:T(8,128)(2,1)S(1)}, bf16[160,2048]{1,0:T(8,128)(2,1)S(1)}, u32[]{:S(2)}, u32[]{:S(2)}) collective-permute-start(bf16[160,2048]{1,0:T(8,128)(2,1)S(1)} %get-tuple-element.32), channel_id=1, source_target_pairs={{0,28},{4,32},{8,36},{12,40},{16,44},{20,48},{24,52},{28,56},{32,6... | collective-permute-start | bytes 1966088 | tf_op jit(solution)/shard_map/ppermute | solution.py:19
  116.0 10.1 %copy-start.6 = (f32[2048]{0:T(1024)S(1)}, f32[2048]{0:T(1024)}, u32[]{:S(2)}) copy-start(f32[2048]{0:T(1024)} %param.24) | copy-start | bytes 24580
  151.1 10.8 %copy-start.8 = (f32[64]{0:T(128)}, f32[64]{0:T(128)S(1)}, u32[]{:S(2)}) copy-start(f32[64]{0:T(128)S(1)} %multiply_power_fusion) | copy-start | bytes 772
  231.2 7.0 %copy-start.2 = (bf16[640,8192]{1,0:T(8,128)(2,1)S(1)}, bf16[640,8192]{1,0:T(8,128)(2,1)}, u32[]{:S(2)}) copy-start(bf16[640,8192]{1,0:T(8,128)(2,1)} %all-gather.2.cloned.1.call-done) | copy-start | bytes 31457284
  259.3 3.8 %copy-start.3 = (pred[640,640]{0,1:T(8,128)(4,1)S(1)}, pred[640,640]{0,1:T(8,128)(4,1)}, u32[]{:S(2)}) copy-start(pred[640,640]{0,1:T(8,128)(4,1)} %compare_and_fusion) | copy-start | bytes 1228804
  269.6 7.8 %copy-start.16 = (f32[8192]{0:T(1024)S(1)}, f32[8192]{0:T(1024)}, u32[]{:S(2)}) copy-start(f32[8192]{0:T(1024)} %param.20) | copy-start | bytes 98308
  269.6 7.8 %copy-start.18 = (f32[1024]{0:T(1024)S(1)}, f32[1024]{0:T(1024)}, u32[]{:S(2)}) copy-start(f32[1024]{0:T(1024)} %param.25) | copy-start | bytes 12292
  277.4 39.0 %copy-start.9 = (s32[8]{0:T(128)S(1)}, s32[8]{0:T(128)}, u32[]{:S(2)}) copy-start(s32[8]{0:T(128)} %param.15) | copy-start | bytes 100
  277.4 39.0 %copy-start.10 = (pred[8]{0:T(512)(128)(4,1)S(1)}, pred[8]{0:T(512)(128)(4,1)}, u32[]{:S(2)}) copy-start(pred[8]{0:T(512)(128)(4,1)} %iota_compare_fusion.3) | copy-start | bytes 28
  277.5 39.0 %copy-start.11 = (pred[8]{0:T(512)(128)(4,1)S(1)}, pred[8]{0:T(512)(128)(4,1)}, u32[]{:S(2)}) copy-start(pred[8]{0:T(512)(128)(4,1)} %iota_compare_fusion.4) | copy-start | bytes 28
  277.5 39.0 %copy-start.12 = (pred[8]{0:T(512)(128)(4,1)S(1)}, pred[8]{0:T(512)(128)(4,1)}, u32[]{:S(2)}) copy-start(pred[8]{0:T(512)(128)(4,1)} %iota_compare_fusion.5) | copy-start | bytes 28
  277.5 39.0 %copy-start.13 = (pred[8]{0:T(512)(128)(4,1)S(1)}, pred[8]{0:T(512)(128)(4,1)}, u32[]{:S(2)}) copy-start(pred[8]{0:T(512)(128)(4,1)} %iota_compare_fusion.6) | copy-start | bytes 28
  277.5 39.0 %copy-start.14 = (pred[8]{0:T(512)(128)(4,1)S(1)}, pred[8]{0:T(512)(128)(4,1)}, u32[]{:S(2)}) copy-start(pred[8]{0:T(512)(128)(4,1)} %iota_compare_fusion.7) | copy-start | bytes 28
  277.5 39.0 %copy-start.15 = (pred[8]{0:T(512)(128)(4,1)S(1)}, pred[8]{0:T(512)(128)(4,1)}, u32[]{:S(2)}) copy-start(pred[8]{0:T(512)(128)(4,1)} %iota_compare_fusion.8) | copy-start | bytes 28
  277.5 39.2 %copy-start.17 = (f32[8,160]{1,0:T(8,128)S(1)}, f32[8,160]{1,0:T(8,128)}, u32[]{:S(2)}) copy-start(f32[8,160]{1,0:T(8,128)} %param.14) | copy-start | bytes 15364
  277.5 39.1 %copy-start.19 = (s32[160]{0:T(256)S(1)}, s32[160]{0:T(256)}, u32[]{:S(2)}) copy-start(s32[160]{0:T(256)} %iota_add_fusion) | copy-start | bytes 1924
  277.5 40.0 %copy-start.1 = (bf16[8192,128]{1,0:T(8,128)(2,1)S(1)}, bf16[8192,128]{1,0:T(8,128)(2,1)}, u32[]{:S(2)}) copy-start(bf16[8192,128]{1,0:T(8,128)(2,1)} %param.22) | copy-start | bytes 6291460
  299.8 12.9 %collective-permute-start.13 = (f32[160]{0:T(256)S(1)}, f32[160]{0:T(256)S(1)}, u32[]{:S(2)}, u32[]{:S(2)}) collective-permute-start(f32[160]{0:T(256)S(1)} %get-tuple-element.52), channel_id=1, source_target_pairs={{0,124},{4,0},{8,4},{12,8},{16,12},{20,16},{24,20},{28,24},{32,28}... | collective-permute-start | bytes 1928 | tf_op jit(solution)/shard_map/ppermute | solution.py:19
  302.7 10.4 %collective-permute-start.12 = (f32[160]{0:T(256)S(1)}, f32[160]{0:T(256)S(1)}, u32[]{:S(2)}, u32[]{:S(2)}) collective-permute-start(f32[160]{0:T(256)S(1)} %get-tuple-element.51), channel_id=1, source_target_pairs={{0,120},{4,124},{8,0},{12,4},{16,8},{20,12},{24,16},{28,20},{32,24... | collective-permute-start | bytes 1928 | tf_op jit(solution)/shard_map/ppermute | solution.py:19
  308.3 6.3 %collective-permute-start.11 = (f32[160]{0:T(256)S(1)}, f32[160]{0:T(256)S(1)}, u32[]{:S(2)}, u32[]{:S(2)}) collective-permute-start(f32[160]{0:T(256)S(1)} %get-tuple-element.50), channel_id=1, source_target_pairs={{0,116},{4,120},{8,124},{12,0},{16,4},{20,8},{24,12},{28,16},{32,2... | collective-permute-start | bytes 1928 | tf_op jit(solution)/shard_map/ppermute | solution.py:19
  309.2 5.4 %collective-permute-start.10 = (f32[160]{0:T(256)S(1)}, f32[160]{0:T(256)S(1)}, u32[]{:S(2)}, u32[]{:S(2)}) collective-permute-start(f32[160]{0:T(256)S(1)} %get-tuple-element.49), channel_id=1, source_target_pairs={{0,112},{4,116},{8,120},{12,124},{16,0},{20,4},{24,8},{28,12},{32,... | collective-permute-start | bytes 1928 | tf_op jit(solution)/shard_map/ppermute | solution.py:19
  309.5 5.1 %collective-permute-start.9 = (f32[160]{0:T(256)S(1)}, f32[160]{0:T(256)S(1)}, u32[]{:S(2)}, u32[]{:S(2)}) collective-permute-start(f32[160]{0:T(256)S(1)} %get-tuple-element.48), channel_id=1, source_target_pairs={{0,108},{4,112},{8,116},{12,120},{16,124},{20,0},{24,4},{28,8},{32... | collective-permute-start | bytes 1928 | tf_op jit(solution)/shard_map/ppermute | solution.py:19
  312.6 3.7 %collective-permute-start.8 = (f32[160]{0:T(256)S(1)}, f32[160]{0:T(256)S(1)}, u32[]{:S(2)}, u32[]{:S(2)}) collective-permute-start(f32[160]{0:T(256)S(1)} %get-tuple-element.47), channel_id=1, source_target_pairs={{0,104},{4,108},{8,112},{12,116},{16,120},{20,124},{24,0},{28,4},{... | collective-permute-start | bytes 1928 | tf_op jit(solution)/shard_map/ppermute | solution.py:19
  313.1 3.3 %collective-permute-start.7 = (f32[160]{0:T(256)S(1)}, f32[160]{0:T(256)S(1)}, u32[]{:S(2)}, u32[]{:S(2)}) collective-permute-start(f32[160]{0:T(256)S(1)} %get-tuple-element.46), channel_id=1, source_target_pairs={{0,100},{4,104},{8,108},{12,112},{16,116},{20,120},{24,124},{28,0}... | collective-permute-start | bytes 1928 | tf_op jit(solution)/shard_map/ppermute | solution.py:19
  316.6 0.9 copy-start.5
Sparse Core Ops, SparseCore 0:
  130.4 100.8 all-gather.1

commit v2 on v1

v2 whole, which is shorter than its diff:
```python
import math

import jax
import jax.numpy as jnp
import numpy as np
from jax import lax
from jax.experimental import pallas as pl
from jax.experimental.pallas import tpu as pltpu
from jax.sharding import PartitionSpec as P

MESH = pl.DeviceIdType.MESH
F32 = jnp.float32
BF16 = jnp.bfloat16

HD = 128
EPSILON = 1e-05
DISCOUNT = 0.99
SMOOTHING = 0.95
ROPE_BASE = 500000.0

SHARDS = 32
PLANES = 4
STEPS = 8
SLOT = 160
PACK = 640
TILE = 128
TILES = PACK // TILE
WIDTH = 256
CHUNKS = 8
HEADS = 8
COLS = HEADS * HD + 2 * HD
BAND = SLOT + TILE
LANES = 256
BEFORE = 4
HALF = PACK // 2
PLANE_OF = (0, -1, 1, 2)

CONTRACT_LAST = (((1,), (1,)), ((), ()))


def dot_last(a, b):
    return lax.dot_general(a, b, CONTRACT_LAST, preferred_element_type=F32)


def thirds(value):
    high = value.astype(BF16)
    rest = value - high.astype(F32)
    middle = rest.astype(BF16)
    return high, middle, (rest - middle.astype(F32)).astype(BF16)


def wide_row(ref, row):
    return jnp.concatenate([ref[pl.ds(2 * row + i, 1), :] for i in range(2)], axis=1)


def sum_of_thirds(stacked):
    rows = stacked.shape[0] // 3
    return stacked[:rows] + stacked[rows : 2 * rows] + stacked[2 * rows :]


def kernel(
    lengths,
    dest_shard,
    source_owner,
    pack_offset,
    segments,
    gain,
    value_head,
    folded_head,
    frequency,
    rewards,
    hidden,
    w_query,
    w_key,
    w_value,
    values_out,
    advantages_out,
    first_slots,
    slots,
    outbox,
    inbox,
    weights,
    rows,
    total,
    squares,
    head_terms,
    select,
    cosines,
    sines,
    picks_out,
    picks,
    query_rot,
    key_rot,
    value_rows,
    packed_values,
    by_plane,
    by_step,
    arrived,
    padded_rewards,
    slot_sem,
    weight_sem,
    pick_sem,
    send_sem,
    recv_sem,
    ring_send,
    ring_recv,
    pass_send,
    pass_recv,
    plane_send,
    plane_recv,
    back_send,
    back_recv,
):
    dp = lax.axis_index("dp")
    mp = lax.axis_index("mp")

    def along_dp(by):
        return lax.rem(dp + (by + SHARDS), SHARDS), mp

    def along_mp(by):
        return dp, lax.rem(mp + (by + PLANES), PLANES)

    barrier = pltpu.get_barrier_semaphore()
    peers = [along_dp(by) for by in range(-BEFORE, BEFORE + 1) if by]
    peers += [along_mp(by) for by in (1, -1, 2)]
    for peer in peers:
        pl.semaphore_signal(barrier, inc=1, device_id=peer, device_id_type=MESH)

    def slot_copy(chunk):
        columns = pl.ds(chunk * WIDTH, WIDTH)
        target = first_slots if chunk == 0 else slots.at[chunk - 1]
        return pltpu.make_async_copy(hidden.at[:, :, columns], target, slot_sem.at[chunk])

    weight_copies = [
        pltpu.make_async_copy(source, weights.at[:, :, pl.ds(start, source.shape[2])], weight_sem.at[i])
        for i, (source, start) in enumerate(
            ((w_query, 0), (w_key, HEADS * HD), (w_value, HEADS * HD + HD))
        )
    ]
    for chunk in range(CHUNKS):
        slot_copy(chunk).start()
    for copy in weight_copies:
        copy.start()

    sublanes = lax.broadcasted_iota(jnp.int32, (TILES, TILE), 0)
    lanes = lax.broadcasted_iota(jnp.int32, (TILES, TILE), 1)
    pick = sublanes * TILE + lanes
    segment = segments[...]
    for j in range(STEPS):
        step = lax.rem(dp - source_owner[j] + SHARDS, SHARDS)
        pick = pick + jnp.where(segment == j, step * SLOT - pack_offset[j], 0)
    picks_out[0:TILES, :] = pick
    picks_out[TILES:, :] = jnp.zeros((8 - TILES, TILE), jnp.int32)

    slot_of = []
    for k in range(STEPS):
        shard = lax.rem(dp + k, SHARDS)
        slot = jnp.int32(0)
        for i in range(STEPS):
            slot = jnp.maximum(slot, jnp.where(dest_shard[i] == shard, i, 0))
        slot_of.append(slot)

    def send_copy(chunk, k):
        return pltpu.make_async_remote_copy(
            src_ref=outbox.at[chunk, k],
            dst_ref=inbox.at[chunk, pl.ds(k * SLOT, SLOT)],
            send_sem=send_sem.at[chunk, k],
            recv_sem=recv_sem.at[chunk, k],
            device_id=along_dp(k - BEFORE),
            device_id_type=MESH,
        )

    others = [k for k in range(STEPS) if k != BEFORE]

    def order_slots(chunk, load):
        for k in range(STEPS):
            if k == BEFORE:
                inbox[chunk, k * SLOT : (k + 1) * SLOT, :] = load(slot_of[k])
            else:
                outbox[chunk, k] = load(slot_of[k])

    slot_copy(0).wait()
    order_slots(0, lambda slot: first_slots[slot])

    pl.semaphore_wait(barrier, len(peers))

    pick_copy = pltpu.make_async_remote_copy(
        src_ref=picks_out,
        dst_ref=picks,
        send_sem=pick_sem.at[0],
        recv_sem=pick_sem.at[1],
        device_id=along_dp(-BEFORE),
        device_id_type=MESH,
    )
    pick_copy.start()
    for k in others:
        send_copy(0, k).start()
    for chunk in range(1, CHUNKS):
        slot_copy(chunk).wait()

    def send_chunk(chunk, carry):
        order_slots(chunk, lambda slot: slots[chunk - 1, slot])
        for k in others:
            send_copy(chunk, k).start()
        return carry

    lax.fori_loop(1, CHUNKS, send_chunk, 0)

    total[...] = jnp.zeros_like(total)
    squares[...] = jnp.zeros_like(squares)
    head_terms[...] = jnp.zeros_like(head_terms)
    key_rot[0:SLOT, :] = jnp.zeros((SLOT, HD), BF16)
    value_rows[0:SLOT, :] = jnp.zeros((SLOT, HD), BF16)

    pick_copy.wait_recv()
    tile_lanes = lax.broadcasted_iota(jnp.int32, (TILE, TILE), 1)

    def tables(b, carry):
        row = picks[pl.ds(b, 1), :].astype(F32)
        column = jnp.transpose(jnp.broadcast_to(row, (TILE, TILE)))
        at = pl.ds(pl.multiple_of(b * TILE, TILE), TILE)
        for block in range(STEPS * SLOT // TILE):
            hit = column == (tile_lanes + block * TILE).astype(F32)
            select[at, block * TILE : (block + 1) * TILE] = jnp.where(hit, 1.0, 0.0).astype(BF16)
        position = column
        for k in range(1, STEPS):
            position = position - jnp.where(column >= float(k * SLOT), float(SLOT), 0.0)
        angle = position * frequency[...]
        cosines[at, :] = jnp.cos(angle)
        sines[at, :] = jnp.sin(angle) * jnp.where(tile_lanes < HD // 2, -1.0, 1.0)
        return carry

    lax.fori_loop(0, TILES, tables, 0)

    def ring_copy(way, chunk):
        return pltpu.make_async_remote_copy(
            src_ref=rows.at[0, chunk],
            dst_ref=rows.at[1 + way, chunk],
            send_sem=ring_send.at[way, chunk],
            recv_sem=ring_recv.at[way, chunk],
            device_id=along_mp(1 - 2 * way),
            device_id_type=MESH,
        )

    def pass_copy(way, chunk):
        half = pl.ds(way * HALF, HALF)
        return pltpu.make_async_remote_copy(
            src_ref=rows.at[1 + way, chunk, half],
            dst_ref=rows.at[3, chunk, half],
            send_sem=pass_send.at[way, chunk],
            recv_sem=pass_recv.at[way, chunk],
            device_id=along_mp(1 - 2 * way),
            device_id_type=MESH,
        )

    def pack(chunk):
        for k in others:
            send_copy(chunk, k).wait_recv()
        packed = jnp.dot(select[...], inbox[chunk], preferred_element_type=F32).astype(BF16)
        rows[0, chunk] = packed
        parts = thirds(wide_row(value_head, chunk))
        sub = lax.broadcasted_iota(jnp.int32, (8, WIDTH), 0)
        stacked = jnp.zeros((8, WIDTH), F32)
        for i, part in enumerate(parts):
            stacked = jnp.where(sub == i, part.astype(F32), stacked)
        head_terms[...] += dot_last(stacked.astype(BF16), packed)

    def project(part, plane, chunk):
        block = plane * CHUNKS + chunk
        x = rows[part, chunk].astype(F32)
        squared = x * x
        squares[...] += squared[:, :128] + squared[:, 128:]
        scaled = (x * wide_row(gain, block)).astype(BF16)
        for n in range(COLS // WIDTH):
            columns = slice(n * WIDTH, (n + 1) * WIDTH)
            total[:, columns] += jnp.dot(
                scaled, weights[block, :, columns], preferred_element_type=F32
            )

    def advance(t, carry):
        @pl.when(t < CHUNKS)
        def _():
            pack(t)
            ring_copy(0, t).start()
            ring_copy(1, t).start()

        @pl.when(t == 1)
        def _():
            for copy in weight_copies:
                copy.wait()

        @pl.when((t >= 1) & (t <= CHUNKS))
        def _():
            chunk = t - 1
            for way in range(2):
                ring_copy(way, chunk).wait_recv()
                pass_copy(way, chunk).start()

            def near(part, inner):
                plane = lax.rem(mp + part * (3 * part - 5) // 2 + PLANES, PLANES)
                project(part, plane, chunk)
                return inner

            lax.fori_loop(0, 3, near, 0)

        @pl.when(t >= 2)
        def _():
            chunk = t - 2
            for way in range(2):
                pass_copy(way, chunk).wait_recv()
            project(3, lax.rem(mp + 2, PLANES), chunk)

        return carry

    lax.fori_loop(0, CHUNKS + 2, advance, 0)

    query_scale = math.log2(math.e) / math.sqrt(HD)

    def rotate(b, carry):
        at = pl.ds(pl.multiple_of(b * TILE, TILE), TILE)
        below = pl.ds(pl.multiple_of(SLOT + b * TILE, 32), TILE)
        mean = jnp.sum(squares[at, :], axis=1, keepdims=True) / (PLANES * CHUNKS * WIDTH)
        scale = lax.rsqrt(mean + EPSILON)
        cosine, sine = cosines[at, :], sines[at, :]

        def turned(head):
            x = total[at, head * HD : (head + 1) * HD] * scale
            return x * cosine + pltpu.roll(x, HD // 2, 1) * sine

        for head in range(HEADS):
            query_rot[b, head * TILE : (head + 1) * TILE, :] = (turned(head) * query_scale).astype(BF16)
        key_rot[below, :] = turned(HEADS).astype(BF16)
        value_rows[below, :] = (total[at, (HEADS + 1) * HD :] * scale).astype(BF16)
        return carry

    lax.fori_loop(0, TILES, rotate, 0)

    folded = jnp.concatenate([part.astype(F32) for part in thirds(folded_head[...])], axis=0).astype(BF16)
    reach = lax.broadcasted_iota(jnp.int32, (BAND, 2 * TILE), 0) - SLOT
    query_at = lax.rem(lax.broadcasted_iota(jnp.int32, (BAND, 2 * TILE), 1), TILE)
    lane = lax.broadcasted_iota(jnp.int32, (1, TILE), 1)
    step_sub = lax.broadcasted_iota(jnp.int32, (STEPS, TILE), 0)
    time_sub = lax.broadcasted_iota(jnp.int32, (LANES, TILE), 0)
    packed_values[...] = jnp.zeros_like(packed_values)

    def attend(b, carry):
        band = pl.ds(pl.multiple_of(b * TILE, TILE), BAND)
        keys = key_rot[band, :]
        pick_row = picks[pl.ds(b, 1), :]
        step_row = jnp.zeros_like(pick_row)
        for k in range(1, STEPS):
            step_row = step_row + jnp.where(pick_row >= k * SLOT, 1, 0)
        position_row = pick_row - step_row * SLOT
        first = lane - position_row
        first = jnp.concatenate([first, first], axis=1)
        allowed = (reach <= query_at) & (reach >= first)
        through = sum_of_thirds(dot_last(folded, value_rows[band, :]))
        high, low, _ = thirds(through)
        lifted = jnp.concatenate(
            [high.astype(F32), low.astype(F32), jnp.ones((HEADS, BAND), F32)], axis=0
        ).astype(BF16)
        term = jnp.zeros((1, TILE), F32)
        for pair in range(HEADS // 2):
            scores = dot_last(keys, query_rot[b, pair * 2 * TILE : (pair + 1) * 2 * TILE, :])
            scores = jnp.where(allowed, scores, -1e30)
            peak = jnp.max(scores, axis=0, keepdims=True)
            weight = jnp.exp2(scores - peak).astype(BF16)
            sums = jnp.dot(lifted, weight, preferred_element_type=F32)
            for i in range(2):
                head, part = 2 * pair + i, slice(i * TILE, (i + 1) * TILE)
                above = sums[head : head + 1, part] + sums[HEADS + head : HEADS + head + 1, part]
                term = term + above / sums[2 * HEADS : 2 * HEADS + 1, part]
        ends = head_terms[:, pl.ds(pl.multiple_of(b * TILE, TILE), TILE)]
        term = term + (ends[0:1] + ends[1:2] + ends[2:3])
        spread = jnp.where(step_sub == step_row, term, 0.0)
        spread = jnp.concatenate([part.astype(F32) for part in thirds(spread)], axis=0).astype(BF16)
        placed = jnp.where(time_sub == position_row, 1.0, 0.0).astype(BF16)
        packed_values[...] += sum_of_thirds(dot_last(spread, placed))
        return carry

    lax.fori_loop(0, TILES, attend, 0)

    by_plane[mp] = packed_values[...]

    def plane_copy(by):
        return pltpu.make_async_remote_copy(
            src_ref=by_plane.at[mp],
            dst_ref=by_plane.at[mp],
            send_sem=plane_send.at[by - 1],
            recv_sem=plane_recv.at[by - 1],
            device_id=along_mp(by),
            device_id_type=MESH,
        )

    def plane_arrival(by):
        other = along_mp(-by)[1]
        return pltpu.make_async_remote_copy(
            src_ref=by_plane.at[other],
            dst_ref=by_plane.at[other],
            send_sem=plane_send.at[by - 1],
            recv_sem=plane_recv.at[by - 1],
            device_id=along_mp(by),
            device_id_type=MESH,
        )

    for by in range(1, PLANES):
        plane_copy(by).start()
    padded_rewards[...] = jnp.zeros_like(padded_rewards)
    padded_rewards[:, 0:SLOT] = rewards[...]
    for by in range(1, PLANES):
        plane_arrival(by).wait_recv()
    summed = (by_plane[0] + by_plane[1]) + (by_plane[2] + by_plane[3])

    def back_copy(k):
        return pltpu.make_async_remote_copy(
            src_ref=by_step.at[k],
            dst_ref=arrived.at[k],
            send_sem=back_send.at[k],
            recv_sem=back_recv.at[k],
            device_id=along_dp(BEFORE - k),
            device_id_type=MESH,
        )

    for k in range(STEPS):
        one = jnp.broadcast_to(summed[k : k + 1, :], (8, LANES))
        if k == BEFORE:
            arrived[k] = one
        else:
            by_step[k] = one
    for k in others:
        back_copy(k).start()
    for k in others:
        back_copy(k).wait_recv()

    sub = lax.broadcasted_iota(jnp.int32, (STEPS, LANES), 0)
    time = lax.broadcasted_iota(jnp.int32, (STEPS, LANES), 1)
    slot_values = jnp.zeros((STEPS, LANES), F32)
    length = jnp.zeros((STEPS, LANES), jnp.int32)
    for i in range(STEPS):
        step = jnp.minimum(lax.rem(dest_shard[i] - dp + SHARDS, SHARDS), STEPS - 1)
        slot_values = jnp.where(sub == i, arrived[step], slot_values)
        length = jnp.where(sub == i, lengths[i], length)
    live = time < length
    values = jnp.where(live, slot_values, 0.0)
    following = jnp.where(time + 1 < length, pltpu.roll(values, LANES - 1, 1), 0.0)
    advantages = jnp.where(live, padded_rewards[...] + DISCOUNT * following - values, 0.0)
    shift = 1
    while shift < SLOT:
        later = jnp.where(time < LANES - shift, pltpu.roll(advantages, LANES - shift, 1), 0.0)
        advantages = advantages + (DISCOUNT * SMOOTHING) ** shift * later
        shift *= 2
    values_out[...] = values[:, 0:SLOT]
    advantages_out[...] = advantages[:, 0:SLOT]

    pick_copy.wait_send()

    def drain(chunk, carry):
        for k in others:
            send_copy(chunk, k).wait_send()
        for way in range(2):
            ring_copy(way, chunk).wait_send()
            pass_copy(way, chunk).wait_send()
        return carry

    lax.fori_loop(0, CHUNKS, drain, 0)
    for by in range(1, PLANES):
        plane_copy(by).wait_send()
    for k in others:
        back_copy(k).wait_send()


def local(
    hidden,
    rewards,
    lengths,
    dest_shard,
    source_owner,
    pack_offset,
    segment_ids,
    norm_gain,
    w_query,
    w_key,
    w_value,
    value_head,
    folded_head,
):
    blocks = PLANES * CHUNKS
    half = HD // 2
    frequency = (ROPE_BASE ** (-np.arange(half, dtype=np.float64) / half)).astype(np.float32)
    frequency = jnp.asarray(np.concatenate([frequency, frequency])[None, :])
    smem = pl.BlockSpec(memory_space=pltpu.SMEM)
    vmem = pl.BlockSpec(memory_space=pltpu.VMEM)
    hbm = pl.BlockSpec(memory_space=pl.ANY)
    dma = pltpu.SemaphoreType.DMA
    out = jax.ShapeDtypeStruct((STEPS, SLOT), F32)
    return pl.pallas_call(
        kernel,
        name="critic",
        out_shape=(out, out),
        in_specs=[smem] * 4 + [vmem] * 6 + [hbm] * 4,
        out_specs=(vmem, vmem),
        scratch_shapes=[
            pltpu.VMEM((STEPS, SLOT, WIDTH), BF16),
            pltpu.VMEM((CHUNKS - 1, STEPS, SLOT, WIDTH), BF16),
            pltpu.VMEM((CHUNKS, STEPS, SLOT, WIDTH), BF16),
            pltpu.VMEM((CHUNKS, STEPS * SLOT, WIDTH), BF16),
            pltpu.VMEM((blocks, WIDTH, COLS), BF16),
            pltpu.VMEM((PLANES, CHUNKS, PACK, WIDTH), BF16),
            pltpu.VMEM((PACK, COLS), F32),
            pltpu.VMEM((PACK, 128), F32),
            pltpu.VMEM((8, PACK), F32),
            pltpu.VMEM((PACK, STEPS * SLOT), BF16),
            pltpu.VMEM((PACK, HD), F32),
            pltpu.VMEM((PACK, HD), F32),
            pltpu.VMEM((8, TILE), jnp.int32),
            pltpu.VMEM((8, TILE), jnp.int32),
            pltpu.VMEM((TILES, HEADS * TILE, HD), BF16),
            pltpu.VMEM((SLOT + PACK, HD), BF16),
            pltpu.VMEM((SLOT + PACK, HD), BF16),
            pltpu.VMEM((STEPS, LANES), F32),
            pltpu.VMEM((PLANES, STEPS, LANES), F32),
            pltpu.VMEM((STEPS, 8, LANES), F32),
            pltpu.VMEM((STEPS, 8, LANES), F32),
            pltpu.VMEM((STEPS, LANES), F32),
            dma((CHUNKS,)),
            dma((3,)),
            dma((2,)),
            dma((CHUNKS, STEPS)),
            dma((CHUNKS, STEPS)),
            dma((2, CHUNKS)),
            dma((2, CHUNKS)),
            dma((2, CHUNKS)),
            dma((2, CHUNKS)),
            dma((3,)),
            dma((3,)),
            dma((STEPS,)),
            dma((STEPS,)),
        ],
        compiler_params=pltpu.CompilerParams(
            collective_id=0, has_side_effects=True, vmem_limit_bytes=67_043_328
        ),
    )(
        lengths,
        dest_shard,
        source_owner,
        pack_offset,
        segment_ids.reshape(TILES, TILE),
        norm_gain.reshape(2 * blocks, 128),
        value_head.reshape(2 * CHUNKS, 128),
        folded_head.reshape(HEADS, HD),
        frequency,
        rewards,
        hidden.reshape(STEPS, SLOT, CHUNKS * WIDTH),
        w_query.reshape(blocks, WIDTH, HEADS * HD),
        w_key.reshape(blocks, WIDTH, HD),
        w_value.reshape(blocks, WIDTH, HD),
    )


def solution(mesh):
    return jax.shard_map(
        local,
        mesh=mesh,
        in_specs=(
            P("dp", "mp"),
            P("dp", None),
            P("dp"),
            P("dp"),
            P("dp"),
            P("dp"),
            P("dp"),
            P(),
            P(None, "mp"),
            P(None, "mp"),
            P(None, "mp"),
            P("mp"),
            P("mp"),
        ),
        out_specs=(P("dp", None), P("dp", None)),
        check_vma=False,
    )
```

time: 325 us -> 129 us (0.40)
  waiting for transfers between devices: 149 us -> 0 us
  Pallas kernels: 0 us -> 126 us
  other arithmetic: 42 us -> 0 us
  matrix products: 41.8 us -> 0 us
  between operations: 34.6 us -> 0.64 us
  starting transfers between devices: 27 us -> 0 us
  local copies, waits for them, and re-layouts: 22.7 us -> 2.59 us
  blocking collectives: 7.21 us -> 0 us
    pallas_call x0 -> x1, Pallas kernels: none -> 126 us  [local(): pl.pallas_call(kernel, name='critic', out_shape=(out, out), in_specs=[sme...]
    ppermute x14 -> x0, waiting for transfers between devices: 79.7 us -> none  [passed_along(): lax.ppermute(value, axis, [(i, (i + by) % length) for i in range(length)])]
    all_gather x1 -> x0, waiting for transfers between devices: 69.3 us -> none  [local(): packed = lax.all_gather(own_part, 'mp', axis=1, tiled=True)]
    dot_general x5 -> x0, matrix products: 41.8 us -> none  [the longest x1 14.9 us: head_values(): jnp.einsum('hgqk,khd->qhgd', weights, value_rows, preferred_element_type=...]
    ppermute x14 -> x0, starting transfers between devices: 27 us -> none  [passed_along(): lax.ppermute(value, axis, [(i, (i + by) % length) for i in range(length)])]
    reduce_sum x6 -> x0, other arithmetic: 26 us -> none  [the longest x1 7.83 us: head_values(): row_total = jnp.sum(exp_scores, axis=-1, keepdims=True)]
    gather x1 -> x0, local copies, waits for them, and re-layouts: 10.1 us -> none  [local(): own_part = jnp.take(jnp.concatenate(received, axis=0), pick_rows, axis=0)]
    eq x8 -> x0, other arithmetic: 8.29 us -> none  [local(): slot_lanes == slot_for(shift_by)]
  transfers between devices with their start and end apart: 15 -> 0, of which waited for: 9 -> 0; matrix products, arithmetic and copies ran while one was open for 7% -> 0% of each run, Pallas kernels for 0% -> 0%
where the time goes in v2:
time: 129 us
  Pallas kernels  126 us (98%)
  local copies, waits for them, and re-layouts  2.59 us (2%)
    pallas_call x1, Pallas kernels, local(): pl.pallas_call(kernel, name='critic', out_shape=(out, out), in_specs=[sme...  126 us
    unnamed x2, local copies, waits for them, and re-layouts  2.59 us

profile of v2, /device:TPU:1, one launch (start us, length us, event | category | flops | bytes accessed | tf_op | source)
XLA Modules:
  0.0 129.1 jit_solution(12870841600481451525)
XLA Ops:
  0.6 125.9 %critic.1 = (f32[8,160]{1,0:T(8,128)}, f32[8,160]{1,0:T(8,128)}) custom-call(s32[8]{0:T(128)} %lengths.1, s32[8]{0:T(128)} %dest_shard.1, s32[8]{0:T(128)} %source_owner.1, s32[8]{0:T(128)} %pack_offset.1, s32[5,128]{1,0:T(8,128)} %bitcast.14, f32[64,128]{1,0:T(8,128)} %bitcast.12, f32[16,128]{1,0:T(8,128)} %bitcast.13, f32[8,128]{1,0:T(8,128)} %bitcast.15, ...), custom_call_target="tpu_custom_call" | custom-call | tf_op jit(solution)/shard_map/critic/pallas_call | solution.py:496
  126.6 1.3 %copy.18 = f32[8,160]{1,0:T(8,128)} copy(f32[8,160]{1,0:T(8,128)} %get-tuple-element.4) | data formatting | bytes 10240
  127.9 1.3 %copy.19 = f32[8,160]{1,0:T(8,128)} copy(f32[8,160]{1,0:T(8,128)} %get-tuple-element.5) | data formatting | bytes 10240

commit v3 on v2

v3 whole, which is shorter than its diff:
```python
import math

import jax
import jax.numpy as jnp
import numpy as np
from jax import lax
from jax.experimental import pallas as pl
from jax.experimental.pallas import tpu as pltpu
from jax.sharding import PartitionSpec as P

MESH = pl.DeviceIdType.MESH
F32 = jnp.float32
BF16 = jnp.bfloat16

HD = 128
EPSILON = 1e-05
DISCOUNT = 0.99
SMOOTHING = 0.95
ROPE_BASE = 500000.0

SHARDS = 32
PLANES = 4
STEPS = 8
SLOT = 160
PACK = 640
TILE = 128
TILES = PACK // TILE
WIDTH = 256
CHUNKS = 8
HEADS = 8
COLS = HEADS * HD + 2 * HD
BAND = SLOT + TILE
LANES = 256
BEFORE = 4
HALF = PACK // 2


CONTRACT_LAST = (((1,), (1,)), ((), ()))


def dot_last(a, b):
    return lax.dot_general(a, b, CONTRACT_LAST, preferred_element_type=F32)


def thirds(value):
    high = value.astype(BF16)
    rest = value - high.astype(F32)
    middle = rest.astype(BF16)
    return high, middle, (rest - middle.astype(F32)).astype(BF16)


def wide_row(ref, row):
    return jnp.concatenate([ref[pl.ds(2 * row + i, 1), :] for i in range(2)], axis=1)


def sum_of_thirds(stacked):
    rows = stacked.shape[0] // 3
    return stacked[:rows] + stacked[rows : 2 * rows] + stacked[2 * rows :]


def kernel(
    lengths,
    dest_shard,
    gain,
    value_head,
    folded_head,
    frequency,
    rewards,
    hidden,
    w_query,
    w_key,
    w_value,
    both_out,
    first_slots,
    slots,
    outbox,
    inbox,
    weights,
    rows,
    total,
    squares,
    head_terms,
    select,
    cosines,
    sines,
    sizes_out,
    sizes,
    query_rot,
    key_rot,
    value_rows,
    by_plane,
    by_step,
    arrived,
    padded_rewards,
    slot_sem,
    weight_sem,
    size_send,
    size_recv,
    send_sem,
    recv_sem,
    ring_send,
    ring_recv,
    pass_send,
    pass_recv,
    plane_send,
    plane_recv,
    back_send,
    back_recv,
):
    dp = lax.axis_index("dp")
    mp = lax.axis_index("mp")

    def along_dp(by):
        return lax.rem(dp + (by + SHARDS), SHARDS), mp

    def along_mp(by):
        return dp, lax.rem(mp + (by + PLANES), PLANES)

    barrier = pltpu.get_barrier_semaphore()
    peers = [along_dp(by) for by in range(-BEFORE, BEFORE + 1) if by]
    peers += [along_mp(by) for by in (1, -1, 2)]
    for peer in peers:
        pl.semaphore_signal(barrier, inc=1, device_id=peer, device_id_type=MESH)

    def slot_copy(chunk):
        columns = pl.ds(chunk * WIDTH, WIDTH)
        target = first_slots if chunk == 0 else slots.at[chunk - 1]
        return pltpu.make_async_copy(hidden.at[:, :, columns], target, slot_sem.at[chunk])

    weight_copies = [
        pltpu.make_async_copy(source, weights.at[:, :, pl.ds(start, source.shape[2])], weight_sem.at[i])
        for i, (source, start) in enumerate(
            ((w_query, 0), (w_key, HEADS * HD), (w_value, HEADS * HD + HD))
        )
    ]
    for chunk in range(CHUNKS):
        slot_copy(chunk).start()
    for copy in weight_copies:
        copy.start()

    slot_of = []
    for k in range(STEPS):
        shard = lax.rem(dp + k, SHARDS)
        slot, length = jnp.int32(0), jnp.int32(0)
        for i in range(STEPS):
            here = dest_shard[i] == shard
            slot = jnp.maximum(slot, jnp.where(here, i, 0))
            length = jnp.maximum(length, jnp.where(here, lengths[i], 0))
        slot_of.append(slot)
        tile = jnp.zeros((8, 128), jnp.int32) + length
        if k == BEFORE:
            sizes[k] = tile
        else:
            sizes_out[k] = tile

    def size_copy(k):
        return pltpu.make_async_remote_copy(
            src_ref=sizes_out.at[k],
            dst_ref=sizes.at[k],
            send_sem=size_send.at[k],
            recv_sem=size_recv.at[k],
            device_id=along_dp(k - BEFORE),
            device_id_type=MESH,
        )

    def send_copy(chunk, k):
        return pltpu.make_async_remote_copy(
            src_ref=outbox.at[chunk, k],
            dst_ref=inbox.at[chunk, pl.ds(k * SLOT, SLOT)],
            send_sem=send_sem.at[chunk, k],
            recv_sem=recv_sem.at[chunk, k],
            device_id=along_dp(k - BEFORE),
            device_id_type=MESH,
        )

    others = [k for k in range(STEPS) if k != BEFORE]

    def order_slots(chunk, load):
        for k in range(STEPS):
            if k == BEFORE:
                inbox[chunk, k * SLOT : (k + 1) * SLOT, :] = load(slot_of[k])
            else:
                outbox[chunk, k] = load(slot_of[k])

    slot_copy(0).wait()
    order_slots(0, lambda slot: first_slots[slot])

    pl.semaphore_wait(barrier, len(peers))

    for k in others:
        size_copy(k).start()
    for k in others:
        send_copy(0, k).start()
    for chunk in range(1, CHUNKS):
        slot_copy(chunk).wait()

    def send_chunk(chunk, carry):
        order_slots(chunk, lambda slot: slots[chunk - 1, slot])
        for k in others:
            send_copy(chunk, k).start()
        return carry

    lax.fori_loop(1, CHUNKS, send_chunk, 0)

    total[...] = jnp.zeros_like(total)
    squares[...] = jnp.zeros_like(squares)
    head_terms[...] = jnp.zeros_like(head_terms)
    key_rot[0:SLOT, :] = jnp.zeros((SLOT, HD), BF16)
    value_rows[0:SLOT, :] = jnp.zeros((SLOT, HD), BF16)

    for k in others:
        size_copy(k).wait_recv()
    size = [sizes[k, 0:1, :] for k in range(STEPS)]
    offset = [jnp.zeros_like(size[0])]
    for k in range(1, STEPS):
        offset.append(offset[-1] + size[k - 1])

    def step_start(row):
        start = jnp.zeros_like(row)
        for k in range(1, STEPS):
            start = jnp.where(row >= offset[k], offset[k], start)
        return start

    packed_row = lax.broadcasted_iota(jnp.int32, (PACK, 128), 0)
    for block in range(STEPS * SLOT // 128):
        column = lax.broadcasted_iota(jnp.int32, (1, 128), 1) + block * 128
        target = jnp.zeros_like(column)
        for k in range(block * 128 // SLOT, (block * 128 + 127) // SLOT + 1):
            position = column - k * SLOT
            row = jnp.where(position < size[k], offset[k] + position, -1)
            target = jnp.where(position >= 0, row, target)
        select[:, block * 128 : (block + 1) * 128] = jnp.where(packed_row == target, 1.0, 0.0).astype(BF16)

    def ring_copy(way, chunk):
        return pltpu.make_async_remote_copy(
            src_ref=rows.at[0, chunk],
            dst_ref=rows.at[1 + way, chunk],
            send_sem=ring_send.at[way, chunk],
            recv_sem=ring_recv.at[way, chunk],
            device_id=along_mp(1 - 2 * way),
            device_id_type=MESH,
        )

    def pass_copy(way, chunk):
        half = pl.ds(way * HALF, HALF)
        return pltpu.make_async_remote_copy(
            src_ref=rows.at[1 + way, chunk, half],
            dst_ref=rows.at[3, chunk, half],
            send_sem=pass_send.at[way, chunk],
            recv_sem=pass_recv.at[way, chunk],
            device_id=along_mp(1 - 2 * way),
            device_id_type=MESH,
        )

    def pack(chunk):
        for k in others:
            send_copy(chunk, k).wait_recv()
        packed = jnp.dot(select[...], inbox[chunk], preferred_element_type=F32)
        rows[0, chunk] = packed.astype(BF16)

    def head_term(chunk):
        parts = thirds(wide_row(value_head, chunk))
        sub = lax.broadcasted_iota(jnp.int32, (8, WIDTH), 0)
        stacked = jnp.zeros((8, WIDTH), F32)
        for i, part in enumerate(parts):
            stacked = jnp.where(sub == i, part.astype(F32), stacked)
        head_terms[...] += dot_last(stacked.astype(BF16), rows[0, chunk])

    def project(source, plane, chunk):
        block = plane * CHUNKS + chunk
        x = rows[source, chunk].astype(F32)
        squared = x * x
        squares[...] += squared[:, :128] + squared[:, 128:]
        scaled = (x * wide_row(gain, block)).astype(BF16)
        for n in range(COLS // WIDTH):
            columns = slice(n * WIDTH, (n + 1) * WIDTH)
            total[:, columns] += jnp.dot(
                scaled, weights[block, :, columns], preferred_element_type=F32
            )

    def ring_start(chunk):
        for way in range(2):
            ring_copy(way, chunk).start()

    pack(0)
    ring_start(0)

    half_sign = jnp.where(lax.broadcasted_iota(jnp.int32, (TILE, TILE), 1) < HD // 2, -1.0, 1.0)
    for b in range(TILES):
        at = slice(b * TILE, (b + 1) * TILE)
        row = lax.broadcasted_iota(jnp.int32, (TILE, TILE), 0) + b * TILE
        angle = (row - step_start(row)).astype(F32) * frequency[...]
        cosines[at, :] = jnp.cos(angle)
        sines[at, :] = jnp.sin(angle) * half_sign

    for copy in weight_copies:
        copy.wait()

    def advance(t, carry):
        @pl.when(t + 1 < CHUNKS)
        def _():
            pack(t + 1)
            ring_start(t + 1)

        @pl.when(t < CHUNKS)
        def _():
            head_term(t)
            project(0, mp, t)
            for way in range(2):
                ring_copy(way, t).wait_recv()
                pass_copy(way, t).start()

            def near(source, inner):
                project(source, lax.rem(mp + 2 * source - 3 + PLANES, PLANES), t)
                return inner

            lax.fori_loop(1, 3, near, 0)

        @pl.when(t >= 1)
        def _():
            for way in range(2):
                pass_copy(way, t - 1).wait_recv()
            project(3, lax.rem(mp + 2, PLANES), t - 1)

        return carry

    lax.fori_loop(0, CHUNKS + 1, advance, 0)

    query_scale = math.log2(math.e) / math.sqrt(HD)

    def rotate(b):
        at = slice(b * TILE, (b + 1) * TILE)
        below = slice(SLOT + b * TILE, SLOT + (b + 1) * TILE)
        mean = jnp.sum(squares[at, :], axis=1, keepdims=True) / (PLANES * CHUNKS * WIDTH)
        scale = lax.rsqrt(mean + EPSILON)
        cosine, sine = cosines[at, :], sines[at, :]

        def turned(head):
            x = total[at, head * HD : (head + 1) * HD] * scale
            return x * cosine + pltpu.roll(x, HD // 2, 1) * sine

        for head in range(HEADS):
            query_rot[b, head * TILE : (head + 1) * TILE, :] = (turned(head) * query_scale).astype(BF16)
        key_rot[below, :] = turned(HEADS).astype(BF16)
        value_rows[below, :] = (total[at, (HEADS + 1) * HD :] * scale).astype(BF16)

    folded = jnp.concatenate([part.astype(F32) for part in thirds(folded_head[...])], axis=0).astype(BF16)
    reach = lax.broadcasted_iota(jnp.int32, (BAND, TILE), 0) - SLOT
    query_at = lax.broadcasted_iota(jnp.int32, (BAND, TILE), 1)
    lane = lax.broadcasted_iota(jnp.int32, (1, TILE), 1)
    step_sub = lax.broadcasted_iota(jnp.int32, (STEPS, TILE), 0)
    time_sub = lax.broadcasted_iota(jnp.int32, (LANES, TILE), 0)

    def attend(b):
        band = slice(b * TILE, b * TILE + BAND)
        keys = key_rot[band, :]
        row = lane + b * TILE
        start = step_start(row)
        step_row = jnp.zeros_like(row)
        for k in range(1, STEPS):
            step_row = step_row + jnp.where(row >= offset[k], 1, 0)
        position_row = row - start
        allowed = (reach <= query_at) & (reach >= start - b * TILE)
        through = sum_of_thirds(dot_last(folded, value_rows[band, :]))
        high, low, _ = thirds(through)
        lifted = jnp.concatenate(
            [high.astype(F32), low.astype(F32), jnp.ones((HEADS, BAND), F32)], axis=0
        ).astype(BF16)
        head_weights = []
        for head in range(HEADS):
            scores = dot_last(keys, query_rot[b, head * TILE : (head + 1) * TILE, :])
            scores = jnp.where(allowed, scores, -1e30)
            peak = jnp.max(scores, axis=0, keepdims=True)
            head_weights.append(jnp.exp2(scores - peak).astype(BF16))
        sums = jnp.dot(lifted, jnp.concatenate(head_weights, axis=1), preferred_element_type=F32)
        ends = head_terms[:, b * TILE : (b + 1) * TILE]
        term = ends[0:1] + ends[1:2] + ends[2:3]
        for head in range(HEADS):
            part = slice(head * TILE, (head + 1) * TILE)
            above = sums[head : head + 1, part] + sums[HEADS + head : HEADS + head + 1, part]
            term = term + above / sums[2 * HEADS : 2 * HEADS + 1, part]
        spread = jnp.where(step_sub == step_row, term, 0.0)
        spread = jnp.concatenate([part.astype(F32) for part in thirds(spread)], axis=0).astype(BF16)
        placed = jnp.where(time_sub == position_row, 1.0, 0.0).astype(BF16)
        return sum_of_thirds(dot_last(spread, placed))

    for b in range(TILES):
        rotate(b)
    shares = attend(0)
    for b in range(1, TILES):
        shares = shares + attend(b)

    def back_copy(k):
        return pltpu.make_async_remote_copy(
            src_ref=by_step.at[k],
            dst_ref=arrived.at[k],
            send_sem=back_send.at[k],
            recv_sem=back_recv.at[k],
            device_id=along_dp(BEFORE - k),
            device_id_type=MESH,
        )

    for k in range(STEPS):
        one = jnp.broadcast_to(shares[k : k + 1, :], (8, LANES))
        if k == BEFORE:
            arrived[k] = one
        else:
            by_step[k] = one
    for k in others:
        back_copy(k).start()
    padded_rewards[...] = jnp.zeros_like(padded_rewards)
    padded_rewards[:, 0:SLOT] = rewards[...]
    for k in others:
        back_copy(k).wait_recv()

    sub = lax.broadcasted_iota(jnp.int32, (STEPS, LANES), 0)
    time = lax.broadcasted_iota(jnp.int32, (STEPS, LANES), 1)
    slot_share = jnp.zeros((STEPS, LANES), F32)
    length = jnp.zeros((STEPS, LANES), jnp.int32)
    for i in range(STEPS):
        step = jnp.minimum(lax.rem(dest_shard[i] - dp + SHARDS, SHARDS), STEPS - 1)
        slot_share = jnp.where(sub == i, arrived[step], slot_share)
        length = jnp.where(sub == i, lengths[i], length)

    by_plane[mp] = slot_share

    def plane_copy(by, plane):
        return pltpu.make_async_remote_copy(
            src_ref=by_plane.at[plane],
            dst_ref=by_plane.at[plane],
            send_sem=plane_send.at[by - 1],
            recv_sem=plane_recv.at[by - 1],
            device_id=along_mp(by),
            device_id_type=MESH,
        )

    for by in range(1, PLANES):
        plane_copy(by, mp).start()
    for by in range(1, PLANES):
        plane_copy(by, along_mp(-by)[1]).wait_recv()
    slot_values = (by_plane[0] + by_plane[1]) + (by_plane[2] + by_plane[3])
    live = time < length
    values = jnp.where(live, slot_values, 0.0)
    following = jnp.where(time + 1 < length, pltpu.roll(values, LANES - 1, 1), 0.0)
    advantages = jnp.where(live, padded_rewards[...] + DISCOUNT * following - values, 0.0)
    shift = 1
    while shift < SLOT:
        later = jnp.where(time < LANES - shift, pltpu.roll(advantages, LANES - shift, 1), 0.0)
        advantages = advantages + (DISCOUNT * SMOOTHING) ** shift * later
        shift *= 2
    both_out[0:STEPS, :] = values
    both_out[STEPS:, :] = advantages

    for k in others:
        size_copy(k).wait_send()

    def drain(chunk, carry):
        for k in others:
            send_copy(chunk, k).wait_send()
        for way in range(2):
            ring_copy(way, chunk).wait_send()
            pass_copy(way, chunk).wait_send()
        return carry

    lax.fori_loop(0, CHUNKS, drain, 0)
    for by in range(1, PLANES):
        plane_copy(by, mp).wait_send()
    for k in others:
        back_copy(k).wait_send()


def local(
    hidden,
    rewards,
    lengths,
    dest_shard,
    source_owner,
    pack_offset,
    segment_ids,
    norm_gain,
    w_query,
    w_key,
    w_value,
    value_head,
    folded_head,
):
    blocks = PLANES * CHUNKS
    half = HD // 2
    frequency = (ROPE_BASE ** (-np.arange(half, dtype=np.float64) / half)).astype(np.float32)
    frequency = jnp.asarray(np.concatenate([frequency, frequency])[None, :])
    smem = pl.BlockSpec(memory_space=pltpu.SMEM)
    vmem = pl.BlockSpec(memory_space=pltpu.VMEM)
    hbm = pl.BlockSpec(memory_space=pl.ANY)
    dma = pltpu.SemaphoreType.DMA
    both = pl.pallas_call(
        kernel,
        name="critic",
        out_shape=jax.ShapeDtypeStruct((2 * STEPS, LANES), F32),
        in_specs=[smem] * 2 + [vmem] * 5 + [hbm] * 4,
        out_specs=vmem,
        scratch_shapes=[
            pltpu.VMEM((STEPS, SLOT, WIDTH), BF16),
            pltpu.VMEM((CHUNKS - 1, STEPS, SLOT, WIDTH), BF16),
            pltpu.VMEM((CHUNKS, STEPS, SLOT, WIDTH), BF16),
            pltpu.VMEM((CHUNKS, STEPS * SLOT, WIDTH), BF16),
            pltpu.VMEM((blocks, WIDTH, COLS), BF16),
            pltpu.VMEM((PLANES, CHUNKS, PACK, WIDTH), BF16),
            pltpu.VMEM((PACK, COLS), F32),
            pltpu.VMEM((PACK, 128), F32),
            pltpu.VMEM((8, PACK), F32),
            pltpu.VMEM((PACK, STEPS * SLOT), BF16),
            pltpu.VMEM((PACK, HD), F32),
            pltpu.VMEM((PACK, HD), F32),
            pltpu.VMEM((STEPS, 8, 128), jnp.int32),
            pltpu.VMEM((STEPS, 8, 128), jnp.int32),
            pltpu.VMEM((TILES, HEADS * TILE, HD), BF16),
            pltpu.VMEM((SLOT + PACK, HD), BF16),
            pltpu.VMEM((SLOT + PACK, HD), BF16),
            pltpu.VMEM((PLANES, STEPS, LANES), F32),
            pltpu.VMEM((STEPS, 8, LANES), F32),
            pltpu.VMEM((STEPS, 8, LANES), F32),
            pltpu.VMEM((STEPS, LANES), F32),
            dma((CHUNKS,)),
            dma((3,)),
            dma((STEPS,)),
            dma((STEPS,)),
            dma((CHUNKS, STEPS)),
            dma((CHUNKS, STEPS)),
            dma((2, CHUNKS)),
            dma((2, CHUNKS)),
            dma((2, CHUNKS)),
            dma((2, CHUNKS)),
            dma((3,)),
            dma((3,)),
            dma((STEPS,)),
            dma((STEPS,)),
        ],
        compiler_params=pltpu.CompilerParams(
            collective_id=0, has_side_effects=True, vmem_limit_bytes=67_043_328
        ),
    )(
        lengths,
        dest_shard,
        norm_gain.reshape(2 * blocks, 128),
        value_head.reshape(2 * CHUNKS, 128),
        folded_head.reshape(HEADS, HD),
        frequency,
        rewards,
        hidden.reshape(STEPS, SLOT, CHUNKS * WIDTH),
        w_query.reshape(blocks, WIDTH, HEADS * HD),
        w_key.reshape(blocks, WIDTH, HD),
        w_value.reshape(blocks, WIDTH, HD),
    )
    return both[:STEPS, :SLOT], both[STEPS:, :SLOT]


def solution(mesh):
    return jax.shard_map(
        local,
        mesh=mesh,
        in_specs=(
            P("dp", "mp"),
            P("dp", None),
            P("dp"),
            P("dp"),
            P("dp"),
            P("dp"),
            P("dp"),
            P(),
            P(None, "mp"),
            P(None, "mp"),
            P(None, "mp"),
            P("mp"),
            P("mp"),
        ),
        out_specs=(P("dp", None), P("dp", None)),
        check_vma=False,
    )
```

time: 129 us -> 123 us (0.953); the launches traced: 129 us -> 121 us
  Pallas kernels: 126 us -> 120 us
    pallas_call x1, Pallas kernels: 126 us -> 120 us  [local(): pl.pallas_call(kernel, name='critic', out_shape=jax.ShapeDtypeStruct((2 *...]
    unnamed x2 -> x0, local copies, waits for them, and re-layouts: 2.59 us -> none
    slice x0 -> x1, local copies, waits for them, and re-layouts: none -> 1.32 us  [local(): return (both[:STEPS, :SLOT], both[STEPS:, :SLOT])]
where the time goes in v3:
time: 123 us; the launch traced here: 121 us
  Pallas kernels  120 us (98%)
  local copies, waits for them, and re-layouts  1.32 us (1%)
    pallas_call x1, Pallas kernels, local(): pl.pallas_call(kernel, name='critic', out_shape=jax.ShapeDtypeStruct((2 *...  120 us

profile of v3, /device:TPU:1, one launch (start us, length us, event | category | flops | bytes accessed | tf_op | source)
XLA Modules:
  0.0 121.5 jit_solution(3514533042812219118)
XLA Ops:
  0.6 119.5 %critic.1 = f32[16,256]{1,0:T(8,128)} custom-call(s32[8]{0:T(128)} %lengths.1, s32[8]{0:T(128)} %dest_shard.1, f32[64,128]{1,0:T(8,128)} %bitcast.11, f32[16,128]{1,0:T(8,128)} %bitcast.12, f32[8,128]{1,0:T(8,128)} %bitcast.13, f32[1,128]{1,0:T(1,128)} %constant.2.clone.frequency, f32[8,160]{1,0:T(8,128)} %rewards.1, bf16[8,160,2048]{2,1,0:T(8,128)(2,1)} %bitcast.8, ...), custom_call_target="tpu_custom_call" | custom-call | tf_op jit(solution)/shard_map/critic/pallas_call | solution.py:495
  120.2 1.3 %fusion = (f32[8,160]{1,0:T(8,128)}, f32[8,160]{1,0:T(8,128)}) fusion(f32[16,256]{1,0:T(8,128)} %critic.1), kind=kLoop, calls=%fused_computation | loop fusion | bytes 20480 | tf_op jit(solution)/shard_map/slice | solution.py:554

commit v4 on v3

--- a/solution.py
+++ b/solution.py
@@ -61,16 +61,21 @@
 def kernel(
     lengths,
     dest_shard,
+    gain_in,
+    value_head_in,
+    folded_head_in,
+    frequency_in,
+    rewards_in,
+    hidden,
+    w_query,
+    w_key,
+    w_value,
+    both_out,
     gain,
     value_head,
     folded_head,
     frequency,
     rewards,
-    hidden,
-    w_query,
-    w_key,
-    w_value,
-    both_out,
     first_slots,
     slots,
     outbox,
@@ -88,10 +93,10 @@
     query_rot,
     key_rot,
     value_rows,
-    by_plane,
     by_step,
     arrived,
     padded_rewards,
+    small_sem,
     slot_sem,
     weight_sem,
     size_send,
@@ -102,8 +107,6 @@
     ring_recv,
     pass_send,
     pass_recv,
-    plane_send,
-    plane_recv,
     back_send,
     back_recv,
 ):
@@ -133,8 +136,22 @@
             ((w_query, 0), (w_key, HEADS * HD), (w_value, HEADS * HD + HD))
         )
     ]
+    small_copies = [
+        pltpu.make_async_copy(source, target, small_sem.at[i])
+        for i, (source, target) in enumerate(
+            (
+                (gain_in, gain),
+                (value_head_in, value_head),
+                (folded_head_in, folded_head),
+                (frequency_in, frequency),
+                (rewards_in, rewards),
+            )
+        )
+    ]
     for chunk in range(CHUNKS):
         slot_copy(chunk).start()
+    for copy in small_copies:
+        copy.start()
     for copy in weight_copies:
         copy.start()
 
@@ -284,6 +301,9 @@
 
     pack(0)
     ring_start(0)
+
+    for copy in small_copies:
+        copy.wait()
 
     half_sign = jnp.where(lax.broadcasted_iota(jnp.int32, (TILE, TILE), 1) < HD // 2, -1.0, 1.0)
     for b in range(TILES):
@@ -390,55 +410,38 @@
     for b in range(1, TILES):
         shares = shares + attend(b)
 
-    def back_copy(k):
+    def back_copy(by, k, plane):
         return pltpu.make_async_remote_copy(
             src_ref=by_step.at[k],
-            dst_ref=arrived.at[k],
-            send_sem=back_send.at[k],
-            recv_sem=back_recv.at[k],
-            device_id=along_dp(BEFORE - k),
+            dst_ref=arrived.at[plane, k],
+            send_sem=back_send.at[by, k],
+            recv_sem=back_recv.at[by, k],
+            device_id=(along_dp(BEFORE - k)[0], along_mp(by)[1]),
             device_id_type=MESH,
         )
 
+    remote = [(by, k) for k in range(STEPS) for by in range(PLANES) if by or k != BEFORE]
     for k in range(STEPS):
-        one = jnp.broadcast_to(shares[k : k + 1, :], (8, LANES))
-        if k == BEFORE:
-            arrived[k] = one
-        else:
-            by_step[k] = one
-    for k in others:
-        back_copy(k).start()
+        for half in range(LANES // 128):
+            by_step[k, half : half + 1, :] = shares[k : k + 1, half * 128 : (half + 1) * 128]
+    for by, k in remote:
+        back_copy(by, k, mp).start()
+    arrived[mp, BEFORE] = by_step[BEFORE]
     padded_rewards[...] = jnp.zeros_like(padded_rewards)
     padded_rewards[:, 0:SLOT] = rewards[...]
-    for k in others:
-        back_copy(k).wait_recv()
+    for by, k in remote:
+        back_copy(by, k, along_mp(-by)[1]).wait_recv()
 
     sub = lax.broadcasted_iota(jnp.int32, (STEPS, LANES), 0)
     time = lax.broadcasted_iota(jnp.int32, (STEPS, LANES), 1)
-    slot_share = jnp.zeros((STEPS, LANES), F32)
+    slot_values = jnp.zeros((STEPS, LANES), F32)
     length = jnp.zeros((STEPS, LANES), jnp.int32)
     for i in range(STEPS):
         step = jnp.minimum(lax.rem(dest_shard[i] - dp + SHARDS, SHARDS), STEPS - 1)
-        slot_share = jnp.where(sub == i, arrived[step], slot_share)
+        both = (arrived[0, step] + arrived[1, step]) + (arrived[2, step] + arrived[3, step])
+        line = jnp.concatenate([both[0:1], both[1:2]], axis=1)
+        slot_values = jnp.where(sub == i, line, slot_values)
         length = jnp.where(sub == i, lengths[i], length)
-
-    by_plane[mp] = slot_share
-
-    def plane_copy(by, plane):
-        return pltpu.make_async_remote_copy(
-            src_ref=by_plane.at[plane],
-            dst_ref=by_plane.at[plane],
-            send_sem=plane_send.at[by - 1],
-            recv_sem=plane_recv.at[by - 1],
-            device_id=along_mp(by),
-            device_id_type=MESH,
-        )
-
-    for by in range(1, PLANES):
-        plane_copy(by, mp).start()
-    for by in range(1, PLANES):
-        plane_copy(by, along_mp(-by)[1]).wait_recv()
-    slot_values = (by_plane[0] + by_plane[1]) + (by_plane[2] + by_plane[3])
     live = time < length
     values = jnp.where(live, slot_values, 0.0)
     following = jnp.where(time + 1 < length, pltpu.roll(values, LANES - 1, 1), 0.0)
@@ -463,10 +466,8 @@
         return carry
 
     lax.fori_loop(0, CHUNKS, drain, 0)
-    for by in range(1, PLANES):
-        plane_copy(by, mp).wait_send()
-    for k in others:
-        back_copy(k).wait_send()
+    for by, k in remote:
+        back_copy(by, k, mp).wait_send()
 
 
 def local(
@@ -496,9 +497,14 @@
         kernel,
         name="critic",
         out_shape=jax.ShapeDtypeStruct((2 * STEPS, LANES), F32),
-        in_specs=[smem] * 2 + [vmem] * 5 + [hbm] * 4,
+        in_specs=[smem] * 2 + [hbm] * 9,
         out_specs=vmem,
         scratch_shapes=[
+            pltpu.VMEM((2 * blocks, 128), F32),
+            pltpu.VMEM((2 * CHUNKS, 128), F32),
+            pltpu.VMEM((HEADS, HD), F32),
+            pltpu.VMEM((1, HD), F32),
+            pltpu.VMEM((STEPS, SLOT), F32),
             pltpu.VMEM((STEPS, SLOT, WIDTH), BF16),
             pltpu.VMEM((CHUNKS - 1, STEPS, SLOT, WIDTH), BF16),
             pltpu.VMEM((CHUNKS, STEPS, SLOT, WIDTH), BF16),
@@ -516,10 +522,10 @@
             pltpu.VMEM((TILES, HEADS * TILE, HD), BF16),
             pltpu.VMEM((SLOT + PACK, HD), BF16),
             pltpu.VMEM((SLOT + PACK, HD), BF16),
-            pltpu.VMEM((PLANES, STEPS, LANES), F32),
-            pltpu.VMEM((STEPS, 8, LANES), F32),
-            pltpu.VMEM((STEPS, 8, LANES), F32),
+            pltpu.VMEM((STEPS, LANES // 128, 128), F32),
+            pltpu.VMEM((PLANES, STEPS, LANES // 128, 128), F32),
             pltpu.VMEM((STEPS, LANES), F32),
+            dma((5,)),
             dma((CHUNKS,)),
             dma((3,)),
             dma((STEPS,)),
@@ -530,10 +536,8 @@
             dma((2, CHUNKS)),
             dma((2, CHUNKS)),
             dma((2, CHUNKS)),
-            dma((3,)),
-            dma((3,)),
-            dma((STEPS,)),
-            dma((STEPS,)),
+            dma((PLANES, STEPS)),
+            dma((PLANES, STEPS)),
         ],
         compiler_params=pltpu.CompilerParams(
             collective_id=0, has_side_effects=True, vmem_limit_bytes=67_043_328

time: 123 us -> 121 us (0.984)
  Pallas kernels: 120 us -> 118 us
where the time goes in v4:
time: 121 us; the launch traced here: 120 us
  Pallas kernels  118 us (98%)
  local copies, waits for them, and re-layouts  1.32 us (1%)
    pallas_call x1, Pallas kernels, local(): pl.pallas_call(kernel, name='critic', out_shape=jax.ShapeDtypeStruct((2 *...  118 us

profile of v4, /device:TPU:1, one launch (start us, length us, event | category | flops | bytes accessed | tf_op | source)
XLA Modules:
  0.0 120.4 jit_solution(7597504485205561146)
XLA Ops:
  0.6 118.4 %critic.1 = f32[16,256]{1,0:T(8,128)} custom-call(s32[8]{0:T(128)} %lengths.1, s32[8]{0:T(128)} %dest_shard.1, f32[64,128]{1,0:T(8,128)} %bitcast.11, f32[16,128]{1,0:T(8,128)} %bitcast.12, f32[8,128]{1,0:T(8,128)} %bitcast.13, f32[1,128]{1,0:T(1,128)} %constant.2.clone.frequency_in, f32[8,160]{1,0:T(8,128)} %rewards_in.1, bf16[8,160,2048]{2,1,0:T(8,128)(2,1)} %bitcast.8, ...), custom_call_target="tpu_custom_call" | custom-call | tf_op jit(solution)/shard_map/critic/pallas_call | solution.py:496
  119.1 1.3 %fusion = (f32[8,160]{1,0:T(8,128)}, f32[8,160]{1,0:T(8,128)}) fusion(f32[16,256]{1,0:T(8,128)} %critic.1), kind=kLoop, calls=%fused_computation | loop fusion | bytes 20480 | tf_op jit(solution)/shard_map/slice | solution.py:558

commit v5 on v4

--- a/solution.py
+++ b/solution.py
@@ -33,6 +33,8 @@
 LANES = 256
 BEFORE = 4
 HALF = PACK // 2
+COLUMNS = (slice(0, WIDTH // 2), slice(WIDTH // 2, WIDTH))
+SPLIT = 2
 
 
 CONTRACT_LAST = (((1,), (1,)), ((), ()))
@@ -101,6 +103,10 @@
     weight_sem,
     size_send,
     size_recv,
+    first_send,
+    first_recv,
+    early_send,
+    early_recv,
     send_sem,
     recv_sem,
     ring_send,
@@ -190,6 +196,16 @@
             device_id_type=MESH,
         )
 
+    def first_copy(chunk, part, k):
+        return pltpu.make_async_remote_copy(
+            src_ref=outbox.at[chunk, k, :, COLUMNS[part]],
+            dst_ref=inbox.at[chunk, pl.ds(k * SLOT, SLOT), COLUMNS[part]],
+            send_sem=first_send.at[chunk, part, k],
+            recv_sem=first_recv.at[chunk, part, k],
+            device_id=along_dp(k - BEFORE),
+            device_id_type=MESH,
+        )
+
     others = [k for k in range(STEPS) if k != BEFORE]
 
     def order_slots(chunk, load):
@@ -206,8 +222,9 @@
 
     for k in others:
         size_copy(k).start()
-    for k in others:
-        send_copy(0, k).start()
+    for part in range(2):
+        for k in others:
+            first_copy(0, part, k).start()
     for chunk in range(1, CHUNKS):
         slot_copy(chunk).wait()
 
@@ -217,7 +234,12 @@
             send_copy(chunk, k).start()
         return carry
 
-    lax.fori_loop(1, CHUNKS, send_chunk, 0)
+    for chunk in range(1, SPLIT):
+        order_slots(chunk, lambda slot: slots[chunk - 1, slot])
+        for part in range(2):
+            for k in others:
+                first_copy(chunk, part, k).start()
+    lax.fori_loop(SPLIT, CHUNKS, send_chunk, 0)
 
     total[...] = jnp.zeros_like(total)
     squares[...] = jnp.zeros_like(squares)
@@ -258,6 +280,16 @@
             device_id_type=MESH,
         )
 
+    def first_ring(chunk, part, way):
+        return pltpu.make_async_remote_copy(
+            src_ref=rows.at[0, chunk, :, COLUMNS[part]],
+            dst_ref=rows.at[1 + way, chunk, :, COLUMNS[part]],
+            send_sem=early_send.at[chunk, part, way],
+            recv_sem=early_recv.at[chunk, part, way],
+            device_id=along_mp(1 - 2 * way),
+            device_id_type=MESH,
+        )
+
     def pass_copy(way, chunk):
         half = pl.ds(way * HALF, HALF)
         return pltpu.make_async_remote_copy(
@@ -269,11 +301,17 @@
             device_id_type=MESH,
         )
 
-    def pack(chunk):
-        for k in others:
-            send_copy(chunk, k).wait_recv()
-        packed = jnp.dot(select[...], inbox[chunk], preferred_element_type=F32)
-        rows[0, chunk] = packed.astype(BF16)
+    def pack(chunk, columns=slice(0, WIDTH)):
+        packed = jnp.dot(select[...], inbox[chunk, :, columns], preferred_element_type=F32)
+        rows[0, chunk, :, columns] = packed.astype(BF16)
+
+    def first_pack(chunk):
+        for part in range(2):
+            for k in others:
+                first_copy(chunk, part, k).wait_recv()
+            pack(chunk, COLUMNS[part])
+            for way in range(2):
+                first_ring(chunk, part, way).start()
 
     def head_term(chunk):
         parts = thirds(wide_row(value_head, chunk))
@@ -295,12 +333,7 @@
                 scaled, weights[block, :, columns], preferred_element_type=F32
             )
 
-    def ring_start(chunk):
-        for way in range(2):
-            ring_copy(way, chunk).start()
-
-    pack(0)
-    ring_start(0)
+    first_pack(0)
 
     for copy in small_copies:
         copy.wait()
@@ -316,35 +349,57 @@
     for copy in weight_copies:
         copy.wait()
 
+    def near(t):
+        for way in range(2):
+            pass_copy(way, t).start()
+
+        def one(source, inner):
+            project(source, lax.rem(mp + 2 * source - 3 + PLANES, PLANES), t)
+            return inner
+
+        lax.fori_loop(1, 3, one, 0)
+
+    first_pack(1)
+    head_term(0)
+    project(0, mp, 0)
+    for part in range(2):
+        for way in range(2):
+            first_ring(0, part, way).wait_recv()
+    near(0)
+
     def advance(t, carry):
         @pl.when(t + 1 < CHUNKS)
         def _():
+            for k in others:
+                send_copy(t + 1, k).wait_recv()
             pack(t + 1)
-            ring_start(t + 1)
+            for way in range(2):
+                ring_copy(way, t + 1).start()
 
         @pl.when(t < CHUNKS)
         def _():
             head_term(t)
             project(0, mp, t)
-            for way in range(2):
-                ring_copy(way, t).wait_recv()
-                pass_copy(way, t).start()
-
-            def near(source, inner):
-                project(source, lax.rem(mp + 2 * source - 3 + PLANES, PLANES), t)
-                return inner
-
-            lax.fori_loop(1, 3, near, 0)
-
-        @pl.when(t >= 1)
-        def _():
-            for way in range(2):
-                pass_copy(way, t - 1).wait_recv()
-            project(3, lax.rem(mp + 2, PLANES), t - 1)
-
+
+            @pl.when(t == 1)
+            def _():
+                for part in range(2):
+                    for way in range(2):
+                        first_ring(1, part, way).wait_recv()
+
+            @pl.when(t >= SPLIT)
+            def _():
+                for way in range(2):
+                    ring_copy(way, t).wait_recv()
+
+            near(t)
+
+        for way in range(2):
+            pass_copy(way, t - 1).wait_recv()
+        project(3, lax.rem(mp + 2, PLANES), t - 1)
         return carry
 
-    lax.fori_loop(0, CHUNKS + 1, advance, 0)
+    lax.fori_loop(1, CHUNKS + 1, advance, 0)
 
     query_scale = math.log2(math.e) / math.sqrt(HD)
 
@@ -381,11 +436,7 @@
             step_row = step_row + jnp.where(row >= offset[k], 1, 0)
         position_row = row - start
         allowed = (reach <= query_at) & (reach >= start - b * TILE)
-        through = sum_of_thirds(dot_last(folded, value_rows[band, :]))
-        high, low, _ = thirds(through)
-        lifted = jnp.concatenate(
-            [high.astype(F32), low.astype(F32), jnp.ones((HEADS, BAND), F32)], axis=0
-        ).astype(BF16)
+        lifted = lifted_all[:, band]
         head_weights = []
         for head in range(HEADS):
             scores = dot_last(keys, query_rot[b, head * TILE : (head + 1) * TILE, :])
@@ -406,6 +457,11 @@
 
     for b in range(TILES):
         rotate(b)
+    through = sum_of_thirds(dot_last(folded, value_rows[...]))
+    high, low, _ = thirds(through)
+    lifted_all = jnp.concatenate(
+        [high.astype(F32), low.astype(F32), jnp.ones((HEADS, SLOT + PACK), F32)], axis=0
+    ).astype(BF16)
     shares = attend(0)
     for b in range(1, TILES):
         shares = shares + attend(b)
@@ -457,12 +513,24 @@
     for k in others:
         size_copy(k).wait_send()
 
+    for chunk in range(SPLIT):
+        for part in range(2):
+            for k in others:
+                first_copy(chunk, part, k).wait_send()
+            for way in range(2):
+                first_ring(chunk, part, way).wait_send()
+
     def drain(chunk, carry):
-        for k in others:
-            send_copy(chunk, k).wait_send()
         for way in range(2):
-            ring_copy(way, chunk).wait_send()
             pass_copy(way, chunk).wait_send()
+
+        @pl.when(chunk >= SPLIT)
+        def _():
+            for k in others:
+                send_copy(chunk, k).wait_send()
+            for way in range(2):
+                ring_copy(way, chunk).wait_send()
+
         return carry
 
     lax.fori_loop(0, CHUNKS, drain, 0)
@@ -530,6 +598,10 @@
             dma((3,)),
             dma((STEPS,)),
             dma((STEPS,)),
+            dma((SPLIT, 2, STEPS)),
+            dma((SPLIT, 2, STEPS)),
+            dma((SPLIT, 2, 2)),
+            dma((SPLIT, 2, 2)),
             dma((CHUNKS, STEPS)),
             dma((CHUNKS, STEPS)),
             dma((2, CHUNKS)),

time: 121 us -> 121 us (level)
  no operation moved by 1% of the time
where the time goes in v5:
time: 121 us
  Pallas kernels  119 us (98%)
  local copies, waits for them, and re-layouts  1.32 us (1%)
    pallas_call x1, Pallas kernels, local(): pl.pallas_call(kernel, name='critic', out_shape=jax.ShapeDtypeStruct((2 *...  119 us

profile of v5, /device:TPU:1, one launch (start us, length us, event | category | flops | bytes accessed | tf_op | source)
XLA Modules:
  0.0 120.7 jit_solution(16295461247559919023)
XLA Ops:
  0.6 118.7 %critic.1 = f32[16,256]{1,0:T(8,128)} custom-call(s32[8]{0:T(128)} %lengths.1, s32[8]{0:T(128)} %dest_shard.1, f32[64,128]{1,0:T(8,128)} %bitcast.11, f32[16,128]{1,0:T(8,128)} %bitcast.12, f32[8,128]{1,0:T(8,128)} %bitcast.13, f32[1,128]{1,0:T(1,128)} %constant.2.clone.frequency_in, f32[8,160]{1,0:T(8,128)} %rewards_in.1, bf16[8,160,2048]{2,1,0:T(8,128)(2,1)} %bitcast.8, ...), custom_call_target="tpu_custom_call" | custom-call | tf_op jit(solution)/shard_map/critic/pallas_call | solution.py:564
  119.3 1.3 %fusion = (f32[8,160]{1,0:T(8,128)}, f32[8,160]{1,0:T(8,128)}) fusion(f32[16,256]{1,0:T(8,128)} %critic.1), kind=kLoop, calls=%fused_computation | loop fusion | bytes 20480 | tf_op jit(solution)/shard_map/slice | solution.py:630
